TPU v7x, 256 devices: a whole 4x4x8 slice. The times are simulated.
256 devices in a mesh: rows: 256 (over z, x, y, core).
Axes of the slice: x: 4, y: 4, z: 8, core: 2. Of those that a mesh axis runs over, the one named last changes fastest.
Arguments:
- right_sides: float32 [131072, 2, 256], P('rows'), may hold values from -6 to 6
- order: int32 [131072], P('rows'), may hold values from 0 to 131071, as said below
- leaf_inverse: float32 [262144, 1024], P('rows')
- basis: float32 [8, 262144, 128], P(None, 'rows')
- capacitance: float32 [8, 256, 128, 128], P(None, 'rows'), as said below
Outputs:
- solution: float32 [131072, 2, 256], P('rows')
Inputs may be any that keep to these rules, and one draw needn't show every extreme that they name: `order`: each aligned block of 512 entries holds every patch index of that block, j * 512 to (j + 1) * 512 - 1, exactly once. capacitance[k, d] is the same matrix for all d with the same d // 2 ** (k + 1).
All inputs are finite; a program needn't handle non-finite values.
Results may differ from a plain program's by a relative error of at most 0.0001.
Values sent between devices are 32-bit elements; how exact they have to be, the bound alone decides.
A program may use at most 128 MiB of HBM per device.

v0:
```python
import jax
import jax.numpy as jnp
from jax import lax
from jax.sharding import PartitionSpec as P

exact = lax.Precision.HIGHEST


def swapped(block, axis, stride):
    count = lax.axis_size(axis)
    route = []
    for low in range(count):
        high = low | 1 << stride
        if high != low and high < count:
            route += [(low, high), (high, low)]
    return lax.ppermute(block, axis, route)


def product(left, right):
    return jnp.dot(left, right, precision=exact, preferred_element_type=jnp.float32)


def project(factor, field):
    return lax.dot_general(
        factor, field, (((0,), (0,)), ((), ())), precision=exact, preferred_element_type=jnp.float32
    )


def owner_split(level, levels):
    return level >= levels // 2 and level < levels - 1


def across(block, level):
    return swapped(block, "rows", level)


def arrange(mine, others, side):
    return jnp.where(
        side == 0, jnp.concatenate([others, mine], 0), jnp.concatenate([mine, others], 0)
    )


def own_rows(block, side, rank):
    return lax.dynamic_slice_in_dim(block, side * rank, rank, 0)


def solve_level(partial_value, level, levels, inverse, device):
    rank = partial_value.shape[0]
    side = device >> level & 1
    if owner_split(level, levels):
        columns = partial_value.shape[1]
        group = min(max(1, 128 // rank), columns >> level)
        piece = jnp.transpose(partial_value).reshape(columns // group, group * rank)
        for bit_index in range(level):
            height = piece.shape[0] // 2
            lower = piece[:height]
            upper = piece[height:]
            upper_side = device >> bit_index & 1 == 1
            outgo = jnp.where(upper_side, lower, upper)
            kept = jnp.where(upper_side, upper, lower)
            piece = kept + swapped(outgo, "rows", bit_index)
        mine = piece.reshape(-1, rank)
        others = across(piece, level).reshape(-1, rank)
        coupled = jnp.where(
            side == 0, jnp.concatenate([others, mine], 1), jnp.concatenate([mine, others], 1)
        )
        solved = lax.dot_general(
            coupled,
            inverse,
            (((1,), (1,)), ((), ())),
            precision=exact,
            preferred_element_type=jnp.float32,
        )
        answer = lax.dynamic_slice_in_dim(solved, side * rank, rank, 1).reshape(-1, group * rank)
        for bit_index in reversed(range(level)):
            arrived = swapped(answer, "rows", bit_index)
            upper_side = device >> bit_index & 1 == 1
            answer = jnp.where(
                upper_side,
                jnp.concatenate([arrived, answer], 0),
                jnp.concatenate([answer, arrived], 0),
            )
        return jnp.transpose(answer.reshape(columns, rank))
    if level == levels - 1:
        blank = jnp.zeros_like(partial_value)
        slotted = jnp.where(
            side == 1,
            jnp.concatenate([partial_value, blank], 0),
            jnp.concatenate([blank, partial_value], 0),
        )
        coupled = lax.psum(slotted, "rows")
    else:
        summed = partial_value
        for bit_index in range(level):
            summed = summed + swapped(summed, "rows", bit_index)
        coupled = arrange(summed, across(summed, level), side)
    return own_rows(product(inverse, coupled), side, rank)


def shards(right_sides, order, leaf_inverse, basis, capacitance):
    device = lax.axis_index("rows")
    patch_dev, components, sides = right_sides.shape
    rank = basis.shape[2] // 2
    levels = basis.shape[0]
    local_order = order - device * patch_dev
    ordered = jnp.take(right_sides, local_order, axis=0).reshape(patch_dev * components, sides)
    current = product(leaf_inverse, ordered)
    for level in range(levels):
        partial_value = project(basis[level, :, rank:], current)
        answer = solve_level(partial_value, level, levels, capacitance[level, 0], device)
        current = current - product(basis[level, :, :rank], answer)
    result = current.reshape(patch_dev, components, sides)
    return jnp.zeros_like(right_sides).at[local_order].set(result)


def solution(mesh):
    return jax.shard_map(
        shards,
        mesh=mesh,
        in_specs=(
            P("rows", None, None),
            P("rows"),
            P("rows", None),
            P(None, "rows", None),
            P(None, "rows", None, None),
        ),
        out_specs=P("rows", None, None),
        check_vma=False,
    )
```

profile of v0, /device:TPU:1, one launch (start us, length us, event | category | flops | bytes accessed | tf_op | source)
XLA Modules:
  0.0 531.6 jit_solution(10912617788060798546)
XLA Ops:
  7.8 2.6 gather_fusion
  11.1 9.1 %fusion.1 = f32[256,1024]{1,0:T(8,128)S(1)} fusion(f32[1024,1024]{1,0:T(8,128)} %param.7, f32[1024,256]{1,0:T(8,128)S(1)} %gather.7, pred[1024]{0:T(1024)(128)(4,1)S(1)} %broadcast_in_dim.24), kind=kOutput, calls=%fused_computation.16 | convolution fusion | flops 3221487616 | bytes 6292480 | tf_op jit(solution)/shard_map/dot_general | solution.py:20
  22.4 3.3 collective-permute-start
  34.2 3.1 collective-permute-done.2
  45.4 3.1 collective-permute-done.4
  49.8 3.4 collective-permute-done.5
  58.8 2.7 collective-permute-start.6
  62.6 3.1 collective-permute-done.7
  67.0 3.4 collective-permute-done.8
  70.5 3.1 collective-permute-done.9
  79.4 3.8 collective-permute-start.10
  84.2 2.6 collective-permute-done.11
  88.2 2.8 collective-permute-done.12
  94.7 2.9 collective-permute-done.14
  98.9 2.7 collective-permute-done.15
  102.8 2.8 collective-permute-done.16
  105.7 2.6 collective-permute-done.17
  108.3 8.1 %collective-permute-start.18 = (f32[64,128]{1,0:T(8,128)S(1)}, f32[64,128]{1,0:T(8,128)S(1)}, u32[]{:S(2)}, u32[]{:S(2)}) collective-permute-start(f32[64,128]{1,0:T(8,128)S(1)} %maximum_select_fusion.11), channel_id=1, source_target_pairs={{0,1},{1,0},{2,3},{3,2},{4,5},{5,4},{6,7},{7,6},{8,9},{9,8},{10,11... | collective-permute-start | bytes 98312 | tf_op jit(solution)/shard_map/ppermute | solution.py:16
  123.2 2.6 collective-permute-done.20
  127.0 2.9 collective-permute-done.21
  133.5 3.0 collective-permute-done.23
  141.4 2.8 collective-permute-done.25
  144.3 2.4 collective-permute-done.26
  148.1 3.0 collective-permute-done.27
  151.0 2.6 collective-permute-done.28
  153.6 10.6 %collective-permute-start.29 = (f32[64,128]{1,0:T(8,128)S(1)}, f32[64,128]{1,0:T(8,128)S(1)}, u32[]{:S(2)}, u32[]{:S(2)}) collective-permute-start(f32[64,128]{1,0:T(8,128)S(1)} %maximum_select_fusion.12), channel_id=1, source_target_pairs={{0,1},{1,0},{2,3},{3,2},{4,5},{5,4},{6,7},{7,6},{8,9},{9,8},{10,11... | collective-permute-start | bytes 98312 | tf_op jit(solution)/shard_map/ppermute | solution.py:16
  171.0 2.6 collective-permute-done.31
  174.8 2.9 collective-permute-done.32
  181.3 3.0 collective-permute-done.34
  207.1 13.2 %collective-permute-start.42 = (f32[64,128]{1,0:T(8,128)S(1)}, f32[64,128]{1,0:T(8,128)S(1)}, u32[]{:S(2)}, u32[]{:S(2)}) collective-permute-start(f32[64,128]{1,0:T(8,128)S(1)} %maximum_select_fusion.13), channel_id=1, source_target_pairs={{0,1},{1,0},{2,3},{3,2},{4,5},{5,4},{6,7},{7,6},{8,9},{9,8},{10,11... | collective-permute-start | bytes 98312 | tf_op jit(solution)/shard_map/ppermute | solution.py:16
  226.3 241.9 %all-reduce.4.cloned.1.call-done = f32[128,256]{1,0:T(8,128)} async-done(((f32[128,256]{1,0:T(8,128)}), f32[128,256]{1,0:T(8,128)}) %all-reduce.4.cloned.1.call-update) | async-done | bytes 131088 | tf_op jit(solution)/shard_map/psum | solution.py:91
  473.7 50.5 %scatter_fusion = f32[512,2,256]{2,1,0:T(2,128)} fusion(f32[512,2,256]{2,1,0:T(2,128)} %broadcast_in_dim.21, s32[512]{0:T(512)S(1)} %get-tuple-element.6, f32[512,2,256]{2,1,0:T(2,128)S(1)} %reshape.120), kind=kCustom, calls=%fused_computation.1 | custom fusion | bytes 3147776 | tf_op jit(solution)/shard_map/scatter | solution.py:113
  (173 shorter events, 108.0 us)
Async XLA Ops:
  6.5 461.6 %all-reduce.4.cloned.1.call-start = ((), (), s32[]{:S(2)}) async-start(), calls=%async_computation | async-start | bytes 262144 | tf_op jit(solution)/shard_map/psum | solution.py:91
  22.4 4.2 collective-permute-start
  33.6 3.7 collective-permute-start.2
  45.3 3.2 collective-permute-start.4
  48.5 4.7 collective-permute-start.5
  58.8 3.6 collective-permute-start.6
  62.5 3.2 collective-permute-start.7
  65.7 4.7 collective-permute-start.8
  70.4 3.2 collective-permute-start.9
  79.4 4.7 collective-permute-start.10
  84.1 2.7 collective-permute-start.11
  86.8 4.3 collective-permute-start.12
  93.6 4.0 collective-permute-start.14
  98.9 2.8 collective-permute-start.15
  101.7 4.0 collective-permute-start.16
  105.7 2.6 collective-permute-start.17
  108.3 9.0 %collective-permute-start.18 = (f32[64,128]{1,0:T(8,128)S(1)}, f32[64,128]{1,0:T(8,128)S(1)}, u32[]{:S(2)}, u32[]{:S(2)}) collective-permute-start(f32[64,128]{1,0:T(8,128)S(1)} %maximum_select_fusion.11), channel_id=1, source_target_pairs={{0,1},{1,0},{2,3},{3,2},{4,5},{5,4},{6,7},{7,6},{8,9},{9,8},{10,11... | collective-permute-start | bytes 98312 | tf_op jit(solution)/shard_map/ppermute | solution.py:16
  123.1 2.7 collective-permute-start.20
  125.8 4.1 collective-permute-start.21
  132.4 4.0 collective-permute-start.23
  140.2 4.0 collective-permute-start.25
  146.7 4.3 collective-permute-start.27
  151.0 2.6 collective-permute-start.28
  153.6 11.5 %collective-permute-start.29 = (f32[64,128]{1,0:T(8,128)S(1)}, f32[64,128]{1,0:T(8,128)S(1)}, u32[]{:S(2)}, u32[]{:S(2)}) collective-permute-start(f32[64,128]{1,0:T(8,128)S(1)} %maximum_select_fusion.12), channel_id=1, source_target_pairs={{0,1},{1,0},{2,3},{3,2},{4,5},{5,4},{6,7},{7,6},{8,9},{9,8},{10,11... | collective-permute-start | bytes 98312 | tf_op jit(solution)/shard_map/ppermute | solution.py:16
  170.9 2.7 collective-permute-start.31
  173.6 4.1 collective-permute-start.32
  180.3 4.0 collective-permute-start.34
  186.8 3.3 collective-permute-start.36
  193.9 4.0 collective-permute-start.38
  200.5 4.0 collective-permute-start.40
  204.5 2.6 collective-permute-start.41
  207.1 14.1 %collective-permute-start.42 = (f32[64,128]{1,0:T(8,128)S(1)}, f32[64,128]{1,0:T(8,128)S(1)}, u32[]{:S(2)}, u32[]{:S(2)}) collective-permute-start(f32[64,128]{1,0:T(8,128)S(1)} %maximum_select_fusion.13), channel_id=1, source_target_pairs={{0,1},{1,0},{2,3},{3,2},{4,5},{5,4},{6,7},{7,6},{8,9},{9,8},{10,11... | collective-permute-start | bytes 98312 | tf_op jit(solution)/shard_map/ppermute | solution.py:16
  (13 other events, 27.7 us)
Sparse Core Ops, SparseCore 0:
  226.4 241.7 all-reduce.3
where the time goes:
time: 541 us; the launch traced here: 532 us
  waiting for transfers between devices  338 us (62%)
  starting transfers between devices  65.8 us (12%)
  local copies, waits for them, and re-layouts  58.7 us (11%)
  matrix products  52.9 us (10%)
  between operations  14.3 us (3%)
    psum x1, waiting for transfers between devices, solve_level(): coupled = lax.psum(slotted, 'rows')  242 us
    ppermute x43, waiting for transfers between devices, swapped(): return lax.ppermute(block, axis, route)  96.2 us
    ppermute x43, starting transfers between devices, swapped(): return lax.ppermute(block, axis, route)  65.8 us
    scatter x1, local copies, waits for them, and re-layouts, shards(): return jnp.zeros_like(right_sides).at[local_order].set(result)  50.5 us
    dot_general x14, matrix products, product(): jnp.dot(left, right, precision=exact, preferred_element_type=jnp.float32)  31.8 us
    dot_general x8, matrix products, project(): lax.dot_general(factor, field, (((0,), (0,)), ((), ())), precision=exact,...  18 us
  transfers between devices with their start and end apart: 44, of which 44 were waited for; matrix products, arithmetic and copies ran while one was open for 0% of the time, Pallas kernels for 0%

commit v1 on v0

v1 whole, which is shorter than its diff:
```python
import functools

import jax
import jax.numpy as jnp
from jax import lax
from jax.experimental import pallas as pl
from jax.experimental.pallas import tpu as pltpu
from jax.sharding import PartitionSpec as P

F32 = jnp.float32
BF16 = jnp.bfloat16
MESH = pl.DeviceIdType.MESH
PACKED = (1, 2, 3, 4, 5, 6, 7, 0)
COPIES = 80
VMEM_BYTES = 56 * 1024 * 1024


def split(x):
    high = x.astype(BF16)
    return high, (x - high.astype(F32)).astype(BF16)


def mm(a, b, transposed=False):
    return lax.dot_general(
        a, b, (((1,), (1 if transposed else 0,)), ((), ())), preferred_element_type=F32
    )


def dot3(a, b, transposed=False):
    return mm(a[0], b[0], transposed) + (
        mm(a[0], b[1], transposed) + mm(a[1], b[0], transposed)
    )


def product(a, b, transposed=False):
    return dot3(split(a), split(b), transposed)


def lanes_of(x):
    return lax.broadcasted_iota(jnp.int32, x.shape, 1)


def swap(x):
    return pltpu.roll(x, 64, 1)


def join(left, right):
    return jnp.where(lanes_of(left) < 64, left, right)


def put(half, side):
    return half if side == 0 else swap(half)


def one_hot(order, first, count):
    rows = lax.broadcasted_iota(jnp.int32, (count, order.shape[1]), 0) + first
    return jnp.where(rows == order, 1.0, 0.0)


def solve_kernel(
    rhs, order, linv, basis, cap,
    field,
    rhs_v, linv_v, basis_v, cap_v,
    uh, ul, wh, wl, uth, utl, fth, ftl, gram,
    pick, xh, xl, gathered, oh, ol,
    qraw, q, q0_in, z0, a_in, za, zt0, qb, b_in, rr, x_in, c_in, z5s, z6s, dx, d_in, ztb,
    c1b, c3b, c5b, c6b, mp, mp_in, pk, pk_in, x4, z8, mx, mz,
    ssem, rsem, lsem,
):
    me = lax.axis_index("rows")
    core = lax.rem(me, 2)
    y = lax.rem(lax.div(me, 2), 4)
    x = lax.rem(lax.div(me, 8), 4)
    z = lax.div(me, 32)
    j = core * 4 + y
    plane = z * 32
    row = plane + x * 8
    cell = y * 2 + core

    def row_device(member):
        return row + lax.rem(member, 4) * 2 + lax.div(member, 4)

    row_members = [lax.rem(j + r, 8) for r in range(1, 8)]
    row_devices = [row_device(m) for m in row_members]
    y_members = [lax.rem(y + r, 4) for r in range(1, 4)]
    y_devices = [row + m * 2 + core for m in y_members]
    x_members = [lax.rem(x + r, 4) for r in range(1, 4)]
    x_devices = [plane + m * 8 + cell for m in x_members]
    z_members = [lax.rem(z + r, 8) for r in range(1, 8)]
    z_devices = [m * 32 + x * 8 + cell for m in z_members]
    other_core = row + y * 2 + (1 - core)

    used = [0]
    started = []

    def send(src, dst, device):
        at = used[0]
        used[0] += 1
        copy = pltpu.make_async_remote_copy(
            src_ref=src,
            dst_ref=dst,
            send_sem=ssem.at[at],
            recv_sem=rsem.at[at],
            device_id=(device,),
            device_id_type=MESH,
        )
        copy.start()
        started.append(copy)
        return copy

    def arrive(copies):
        for copy in copies:
            copy.wait_recv()

    def basis_load(c):
        rows = pl.ds(c * 128, 128)
        return pltpu.make_async_copy(basis.at[:, rows, :], basis_v.at[:, rows, :], lsem.at[c])

    def linv_load(c):
        rows = pl.ds(c * 128, 128)
        return pltpu.make_async_copy(linv.at[rows, :], linv_v.at[rows, :], lsem.at[8 + c])

    for c in range(8):
        basis_load(c).start()
    cap_load = pltpu.make_async_copy(cap, cap_v, lsem.at[16])
    cap_load.start()
    rhs_load = pltpu.make_async_copy(rhs, rhs_v, lsem.at[17])
    rhs_load.start()
    for c in range(8):
        linv_load(c).start()
    own = []
    for at, (level, buffer, node) in enumerate(
        ((1, c1b, lax.div(y, 2)), (3, c3b, lax.div(x, 2)), (5, c5b, lax.div(z, 2)), (6, c6b, lax.div(z, 4)))
    ):
        own.append(pltpu.make_async_copy(cap.at[level], buffer.at[node], lsem.at[18 + at]))
        own[-1].start()

    barrier = pltpu.get_barrier_semaphore()
    partners = row_devices + x_devices + z_devices
    for device in partners:
        pl.semaphore_signal(barrier, inc=1, device_id=(device,), device_id_type=MESH)

    def pack(c, carry):
        start = pl.multiple_of(c * 128, 128)
        rows = pl.ds(start, 128)
        basis_load(c).wait()
        for t in range(4):
            a = basis_v[PACKED[2 * t], rows, :]
            b = basis_v[PACKED[2 * t + 1], rows, :]
            u = join(a, swap(b))
            w = join(swap(a), b)
            cols = slice(128 * t, 128 * t + 128)
            uh[rows, cols], ul[rows, cols] = split(u)
            wh[rows, cols], wl[rows, cols] = split(w)
            uth[cols, rows], utl[cols, rows] = split(u.T)
        return carry

    lax.fori_loop(0, 8, pack, 0)

    pl.semaphore_wait(barrier, len(partners))
    cap_load.wait()
    for copy in own:
        copy.wait()
    c1_copies = [send(cap_v.at[1], c1b.at[lax.div(y, 2)], y_devices[1])]
    c3_copies = [send(cap_v.at[3], c3b.at[lax.div(x, 2)], x_devices[1])]
    c5_copies = [send(cap_v.at[5], c5b.at[lax.div(z, 2)], z_devices[r - 1]) for r in (2, 4, 6)]
    c6_copies = [send(cap_v.at[6], c6b.at[lax.div(z, 4)], z_devices[3])]

    for t, low in ((0, 0), (1, 128), (2, 256), (3, 0)):
        rows = slice(128 * t, 128 * t + 128)
        gram[rows, low:] = dot3((uth[rows, :], utl[rows, :]), (wh[:, low:], wl[:, low:]))

    mp[...] = join(swap(gram[0:32, 0:128]), gram[32:64, 0:128])
    for at, base in ((0, 128), (256, 192)):
        rows = slice(base, base + 64)
        pk[:, at : at + 128] = join(gram[rows, 384:512], gram[rows, 128:256])
        pk[:, at + 128 : at + 256] = gram[rows, 256:384]
    for at, base in ((512, 256), (640, 320)):
        rows = slice(base, base + 64)
        pk[:, at : at + 128] = join(gram[rows, 384:512], gram[rows, 256:384])
    mp_in[j] = mp[...]
    pk_in[j] = pk[pl.ds(pl.multiple_of(8 * j, 8), 8), :]
    mp_copies = [send(mp, mp_in.at[j], d) for d in row_devices]
    pk_copies = [
        send(pk.at[pl.ds(pl.multiple_of(8 * m, 8), 8), :], pk_in.at[j], d)
        for m, d in zip(row_members, row_devices)
    ]

    rhs_load.wait()
    local = order[...] - me * 512
    for b in range(4):
        pick[:, 128 * b : 128 * b + 128] = one_hot(local, 128 * b, 128).T.astype(BF16)
    for c in range(2):
        for half in range(2):
            cols = slice((2 * c + half) * 128, (2 * c + half) * 128 + 128)
            xh[:, cols], xl[:, cols] = split(rhs_v[pl.ds(2 * half + c, 512, stride=4), :])
    for source, target in ((xh, oh), (xl, ol)):
        for b in range(4):
            moved = mm(pick[128 * b : 128 * b + 128, :], source[...])
            for c in range(2):
                for half in range(2):
                    at = (2 * c + half) * 128
                    gathered[half, pl.ds(256 * b + c, 128, stride=2), :] = moved[:, at : at + 128]
        for half in range(2):
            target[:, 128 * half : 128 * half + 128] = gathered[half].astype(BF16)

    def leaf(c, carry):
        start = pl.multiple_of(c * 128, 128)
        rows = pl.ds(start, 128)
        linv_load(c).wait()
        value = dot3(split(linv_v[rows, :]), (oh[...], ol[...]))
        field[0, rows, :] = value[:, :128]
        field[1, rows, :] = value[:, 128:]
        fth[:, rows], ftl[:, rows] = split(value.T)
        return carry

    lax.fori_loop(0, 8, leaf, 0)

    arrive(pk_copies)
    total = pk_in[0]
    for m in range(1, 8):
        total = total + pk_in[m]
    x4[x] = total
    x4_copies = [send(x4.at[x], x4.at[x], d) for d in x_devices]

    for b in range(2):
        rows = slice(128 * b, 128 * b + 128)
        qraw[rows, :] = dot3((fth[rows, :], ftl[rows, :]), (wh[...], wl[...]))

    q0_copies = [send(qraw.at[:, pl.ds(384, 128)], q0_in, other_core)]

    own_rows = pl.ds(pl.multiple_of(8 * j, 8), 8)
    arrive(x4_copies)
    for m in range(4):
        mx[m, own_rows, :] = x4[m, :, 0:256]
    for h in range(2):
        mx[4 + h, own_rows, :] = x4[2 * h, :, 256:512] + x4[2 * h + 1, :, 256:512]
    zs = x4[0, :, 512:] + x4[1, :, 512:] + x4[2, :, 512:] + x4[3, :, 512:]
    z8[z] = zs
    z8_copies = [send(z8.at[z], z8.at[z], d) for d in z_devices]
    mxy_copies = [send(mx.at[:, own_rows, :], mx.at[:, own_rows, :], d) for d in y_devices]

    arrive(q0_copies)
    mine, others = qraw[:, 384:], q0_in[...]
    first = jnp.where(core == 0, mine, others)
    second = jnp.where(core == 0, others, mine)
    pair = join(swap(second), first)
    solved = product(pair, cap_v[0], True)
    solved = jnp.where(core == 0, swap(solved), solved)
    solved = jnp.where(lanes_of(solved) < 64, 0.0, solved)
    z0[...] = solved
    q[...] = qraw[...] - product(solved, gram[384:512, :])

    a_in[j] = q[pl.ds(pl.multiple_of(32 * j, 32), 32), 0:128]
    a_copies = [
        send(q.at[pl.ds(pl.multiple_of(32 * m, 32), 32), pl.ds(0, 128)], a_in.at[j], d)
        for m, d in zip(row_members, row_devices)
    ]
    arrive(z8_copies)
    for m in range(8):
        mz[m, own_rows, :] = z8[m, :, 0:128]
    for p in range(4):
        mz[8 + p, own_rows, :] = z8[2 * p, :, 128:] + z8[2 * p + 1, :, 128:]
    mzy_copies = [send(mz.at[:, own_rows, :], mz.at[:, own_rows, :], d) for d in y_devices]
    arrive(c1_copies)
    arrive(mp_copies)
    m12 = []
    for m in range(4):
        part = mp_in[m] + mp_in[4 + m]
        m12.append(jnp.concatenate([swap(part), part], 0))
    m12 = [jnp.concatenate(m12[2 * h : 2 * h + 2], 0) for h in range(2)]
    arrive(a_copies)
    parts = [a_in[m] + a_in[4 + m] for m in range(4)]
    z1 = [product(join(parts[2 * n + 1], swap(parts[2 * n])), c1b[n], True) for n in range(2)]
    left = [parts[2 * h] + parts[2 * h + 1] - product(z1[h], m12[h]) for h in range(2)]
    z2 = product(join(swap(left[1]), left[0]), cap_v[2], True)
    for m in range(4):
        za[m] = join(put(z1[m // 2], m % 2), put(z2, 1 - m // 2))
    own_cols = pl.ds(pl.multiple_of(32 * j, 32), 32)
    zt0[own_cols, :] = za[y]
    zt_copies = [
        send(za.at[lax.rem(m, 4)], zt0.at[own_cols, :], d)
        for m, d in zip(row_members, row_devices)
    ]
    arrive(mxy_copies)
    core_rows = pl.ds(pl.multiple_of(32 * core, 32), 32)
    mxc_copies = [send(mx.at[:, core_rows, :], mx.at[:, core_rows, :], other_core)]
    arrive(zt_copies)
    qb[...] = q[:, 128:] - product(zt0[...], gram[0:128, 128:])

    b_in[j] = qb[own_cols, :]
    b_copies = [
        send(qb.at[pl.ds(pl.multiple_of(32 * m, 32), 32), :], b_in.at[j], d)
        for m, d in zip(row_members, row_devices)
    ]
    arrive(mzy_copies)
    mzc_copies = [send(mz.at[:, core_rows, :], mz.at[:, core_rows, :], other_core)]
    arrive(b_copies)
    total = b_in[0]
    for m in range(1, 8):
        total = total + b_in[m]
    rr[...] = total
    x_rows = pl.ds(pl.multiple_of(8 * x, 8), 8)
    x_in[x] = rr[x_rows, :]
    x_copies = [
        send(rr.at[pl.ds(pl.multiple_of(8 * m, 8), 8), :], x_in.at[x], d)
        for m, d in zip(x_members, x_devices)
    ]
    arrive(c3_copies)
    arrive(mxc_copies)
    m3 = [jnp.concatenate([mx[2 * n], mx[2 * n + 1]], 0) for n in range(2)]
    m4 = jnp.concatenate([mx[4], mx[5]], 0)
    arrive(x_copies)
    low = [x_in[m, :, 0:128] for m in range(4)]
    z3 = [product(join(low[2 * n + 1], swap(low[2 * n])), c3b[n], True) for n in range(2)]
    y3 = [product(z3[n], m3[n]) for n in range(2)]
    left = [low[2 * h] + low[2 * h + 1] - y3[h][:, :128] for h in range(2)]
    z4 = product(join(swap(left[1]), left[0]), cap_v[4], True)
    taken = y3[0] + y3[1] + product(z4, m4)
    high = x_in[0, :, 128:] + x_in[1, :, 128:] + x_in[2, :, 128:] + x_in[3, :, 128:]
    high = jnp.concatenate([high[:, :128] - taken[:, 128:], high[:, 128:] - taken[:, :128]], 1)

    c_in[z] = high
    c_copies = [send(c_in.at[z], c_in.at[z], d) for d in z_devices]
    for m in range(4):
        dx[m, :, 0:128] = join(put(z3[m // 2], m % 2), put(z4, 1 - m // 2))
    arrive(c5_copies)
    arrive(c6_copies)
    arrive(mzc_copies)
    m5 = [jnp.concatenate([mz[2 * p], mz[2 * p + 1]], 0) for p in range(4)]
    m6 = [jnp.concatenate([mz[8 + 2 * n], mz[9 + 2 * n]], 0) for n in range(2)]
    arrive(c_copies)
    low = [c_in[m, :, 0:128] for m in range(8)]
    top = [c_in[m, :, 128:] for m in range(8)]
    z5 = [product(join(low[2 * p + 1], swap(low[2 * p])), c5b[p], True) for p in range(4)]
    y5 = [product(z5[p], m5[p]) for p in range(4)]
    left = [low[2 * p] + low[2 * p + 1] - y5[p] for p in range(4)]
    z6 = [product(join(swap(left[2 * n + 1]), left[2 * n]), c6b[n], True) for n in range(2)]
    y6 = [product(z6[n], m6[n]) for n in range(2)]
    left = []
    for h in range(2):
        value = top[4 * h] + top[4 * h + 1] + top[4 * h + 2] + top[4 * h + 3]
        left.append(value - y5[2 * h] - y5[2 * h + 1] - y6[h])
    z7 = product(join(left[1], swap(left[0])), cap_v[7], True)
    for p in range(4):
        z5s[p] = z5[p]
    for n in range(2):
        z6s[n] = z6[n]
    side5, side6, side7 = lax.rem(z, 2), lax.rem(lax.div(z, 2), 2), lax.div(z, 4)
    own5 = z5s[lax.div(z, 2)]
    own5 = jnp.where(side5 == 0, own5, swap(own5))
    own6 = z6s[lax.div(z, 4)]
    own6 = jnp.where(side6 == 0, swap(own6), own6)
    own7 = jnp.where(side7 == 0, z7, swap(z7))
    middle = join(own5, own6)
    for m in range(4):
        dx[m, :, 128:256] = middle
        dx[m, :, 256:384] = own7

    d_in[x_rows, :] = dx[x]
    d_copies = [send(dx.at[m], d_in.at[x_rows, :], d) for m, d in zip(x_members, x_devices)]
    arrive(d_copies)
    ztb[own_cols, :] = d_in[...]
    ztb_copies = [send(d_in, ztb.at[own_cols, :], d) for d in row_devices]
    arrive(ztb_copies)
    whole = jnp.concatenate([zt0[...], ztb[:, 0:256], join(ztb[:, 256:], z0[...])], 1)
    qh, ql = split(whole)
    fth[:, 0:512] = qh
    ftl[:, 0:512] = ql

    def update(c, carry):
        rows = pl.ds(pl.multiple_of(c * 128, 128), 128)
        taken = dot3((uh[rows, :], ul[rows, :]), (fth[:, 0:512], ftl[:, 0:512]), True)
        field[0, rows, :] = field[0, rows, :] - taken[:, :128]
        field[1, rows, :] = field[1, rows, :] - taken[:, 128:]
        return carry

    lax.fori_loop(0, 8, update, 0)
    for copy in started:
        copy.wait_send()
    assert used[0] == COPIES


def scatter_kernel(field, order, out):
    local = order[...] - lax.axis_index("rows") * 512
    picks = [one_hot(local, 128 * b, 128).astype(BF16) for b in range(4)]
    for c in range(2):
        value = jnp.concatenate([field[h, pl.ds(c, 512, stride=2), :] for h in range(2)], 1)
        high, low = split(value)
        rest = (value - high.astype(F32) - low.astype(F32)).astype(BF16)
        for b in range(4):
            moved = mm(picks[b], high) + (mm(picks[b], low) + mm(picks[b], rest))
            for h in range(2):
                out[pl.ds(512 * b + 2 * h + c, 128, stride=4), :] = moved[:, 128 * h : 128 * h + 128]


def shards(right_sides, order, leaf_inverse, basis, capacitance):
    rhs = right_sides.reshape(512, 2, 2, 128).transpose(0, 2, 1, 3).reshape(2048, 128)
    order = order.reshape(1, 512)
    any_ref = pl.BlockSpec(memory_space=pl.ANY)
    vmem_ref = pl.BlockSpec(memory_space=pltpu.VMEM)
    v = pltpu.VMEM
    field = pl.pallas_call(
        solve_kernel,
        out_shape=jax.ShapeDtypeStruct((2, 1024, 128), F32),
        in_specs=[any_ref, vmem_ref, any_ref, any_ref, any_ref],
        out_specs=vmem_ref,
        scratch_shapes=[
            v((2048, 128), F32), v((1024, 1024), F32), v((8, 1024, 128), F32), v((8, 128, 128), F32),
            v((1024, 512), BF16), v((1024, 512), BF16), v((1024, 512), BF16), v((1024, 512), BF16),
            v((512, 1024), BF16), v((512, 1024), BF16), v((256, 1024), BF16), v((256, 1024), BF16),
            v((512, 512), F32),
            v((512, 512), BF16), v((512, 512), BF16), v((512, 512), BF16), v((2, 1024, 128), F32),
            v((1024, 256), BF16), v((1024, 256), BF16),
            v((256, 512), F32), v((256, 512), F32), v((256, 128), F32), v((256, 128), F32),
            v((8, 32, 128), F32), v((4, 32, 128), F32), v((256, 128), F32), v((256, 384), F32),
            v((8, 32, 384), F32), v((32, 384), F32), v((4, 8, 384), F32), v((8, 8, 256), F32),
            v((4, 8, 128), F32), v((2, 8, 128), F32), v((4, 8, 384), F32), v((32, 384), F32),
            v((256, 384), F32),
            v((2, 128, 128), F32), v((2, 128, 128), F32), v((4, 128, 128), F32), v((2, 128, 128), F32),
            v((32, 128), F32), v((8, 32, 128), F32), v((64, 768), F32), v((8, 8, 768), F32),
            v((4, 8, 768), F32), v((8, 8, 256), F32),
            v((6, 64, 256), F32), v((12, 64, 128), F32),
            pltpu.SemaphoreType.DMA((COPIES,)), pltpu.SemaphoreType.DMA((COPIES,)),
            pltpu.SemaphoreType.DMA((22,)),
        ],
        compiler_params=pltpu.CompilerParams(
            collective_id=0, has_side_effects=True, vmem_limit_bytes=VMEM_BYTES
        ),
    )(rhs, order, leaf_inverse, basis, capacitance.reshape(8, 128, 128))
    out = pl.pallas_call(
        scatter_kernel,
        out_shape=jax.ShapeDtypeStruct((2048, 128), F32),
        in_specs=[vmem_ref, vmem_ref],
        out_specs=vmem_ref,
        compiler_params=pltpu.CompilerParams(vmem_limit_bytes=16 * 1024 * 1024),
    )(field, order)
    return out.reshape(512, 2, 2, 128).transpose(0, 2, 1, 3).reshape(512, 2, 256)


def solution(mesh):
    return jax.shard_map(
        shards,
        mesh=mesh,
        in_specs=(
            P("rows", None, None),
            P("rows"),
            P("rows", None),
            P(None, "rows", None),
            P(None, "rows", None, None),
        ),
        out_specs=P("rows", None, None),
        check_vma=False,
    )
```

time: 541 us -> 69 us (0.13); the launches traced: 532 us -> 68.9 us
  waiting for transfers between devices: 338 us -> 0 us
  Pallas kernels: 0 us -> 67.6 us
  starting transfers between devices: 65.8 us -> 0 us
  local copies, waits for them, and re-layouts: 58.7 us -> 1.22 us
  matrix products: 52.9 us -> 0 us
  between operations: 14.3 us -> 0.03 us
    psum x1 -> x0, waiting for transfers between devices: 242 us -> none  [solve_level(): coupled = lax.psum(slotted, 'rows')]
    ppermute x43 -> x0, waiting for transfers between devices: 96.2 us -> none  [swapped(): return lax.ppermute(block, axis, route)]
    pallas_call x0 -> x2, Pallas kernels: none -> 67.6 us  [the longest x1 65.6 us: shards(): pl.pallas_call(solve_kernel, out_shape=jax.ShapeDtypeStruct((2, 1024, 128...]
    ppermute x43 -> x0, starting transfers between devices: 65.8 us -> none  [swapped(): return lax.ppermute(block, axis, route)]
    dot_general x25 -> x0, matrix products: 52.9 us -> none  [the longest x14 31.8 us: product(): jnp.dot(left, right, precision=exact, preferred_element_type=jnp.float32)]
    scatter x1 -> x0, local copies, waits for them, and re-layouts: 50.5 us -> none  [shards(): return jnp.zeros_like(right_sides).at[local_order].set(result)]
  transfers between devices with their start and end apart: 44 -> 0, of which waited for: 44 -> 0; matrix products, arithmetic and copies ran while one was open for 0% -> 0% of each run, Pallas kernels for 0% -> 0%
where the time goes in v1:
time: 69 us; the launch traced here: 68.9 us
  Pallas kernels  67.6 us (98%)
  local copies, waits for them, and re-layouts  1.22 us (2%)
    pallas_call x1, Pallas kernels, shards(): pl.pallas_call(solve_kernel, out_shape=jax.ShapeDtypeStruct((2, 1024, 128...  65.6 us
    pallas_call x1, Pallas kernels, shards(): pl.pallas_call(scatter_kernel, out_shape=jax.ShapeDtypeStruct((2048, 128)...  2.02 us

profile of v1, /device:TPU:1, one launch (start us, length us, event | category | flops | bytes accessed | tf_op | source)
XLA Modules:
  0.0 68.9 jit_solution(5038319695659322766)
XLA Ops:
  0.0 0.0 copy-start.1
  0.0 65.6 %shard_map.55.field = f32[2,1024,128]{2,1,0:T(8,128)} custom-call(f32[2048,128]{1,0:T(8,128)} %bitcast.14, s32[1,512]{1,0:T(1,128)} %bitcast.12, f32[1024,1024]{1,0:T(8,128)} %linv.1, f32[8,1024,128]{2,1,0:T(8,128)} %basis.1, f32[8,128,128]{2,1,0:T(8,128)} %bitcast.15), custom_call_target="tpu_custom_call" | custom-call | tf_op jit(solution)/shard_map/pallas_call | solution.py:403
  65.6 0.0 copy-done.1
  65.6 0.0 copy-start
  65.6 1.2 %copy-done = f32[2,1024,128]{2,1,0:T(8,128)S(1)} copy-done((f32[2,1024,128]{2,1,0:T(8,128)S(1)}, f32[2,1024,128]{2,1,0:T(8,128)}, u32[]{:S(2)}) %copy-start) | copy-done | bytes 1048600
  66.8 2.0 %shard_map.56 = f32[2048,128]{1,0:T(8,128)} custom-call(f32[2,1024,128]{2,1,0:T(8,128)S(1)} %copy-done, s32[1,512]{1,0:T(1,128)S(1)} %bitcast.13), custom_call_target="tpu_custom_call" | custom-call | tf_op jit(solution)/shard_map/pallas_call | solution.py:431
Async XLA Ops:
  0.0 65.6 %copy-start.1 = (s32[512]{0:T(512)S(1)}, s32[512]{0:T(512)}, u32[]{:S(2)}) copy-start(s32[512]{0:T(512)} %param.6) | copy-start | bytes 6148
  65.6 1.2 %copy-start = (f32[2,1024,128]{2,1,0:T(8,128)S(1)}, f32[2,1024,128]{2,1,0:T(8,128)}, u32[]{:S(2)}) copy-start(f32[2,1024,128]{2,1,0:T(8,128)} %shard_map.55.field) | copy-start | bytes 3145732

commit v2 on v1

v2 whole, which is shorter than its diff:
```python
import functools

import jax
import jax.numpy as jnp
from jax import lax
from jax.experimental import pallas as pl
from jax.experimental.pallas import tpu as pltpu
from jax.sharding import PartitionSpec as P

F32 = jnp.float32
BF16 = jnp.bfloat16
MESH = pl.DeviceIdType.MESH
PACKED = (1, 2, 3, 4, 5, 6, 7, 0)
COPIES = 65
VMEM_BYTES = 56 * 1024 * 1024


def split(x):
    high = x.astype(BF16)
    return high, (x - high.astype(F32)).astype(BF16)


def mm(a, b, transposed=False):
    return lax.dot_general(
        a, b, (((1,), (1 if transposed else 0,)), ((), ())), preferred_element_type=F32
    )


def dot3(a, b, transposed=False):
    return mm(a[0], b[0], transposed) + (
        mm(a[0], b[1], transposed) + mm(a[1], b[0], transposed)
    )


def product(a, b, transposed=False):
    return dot3(split(a), split(b), transposed)


def lanes_of(x):
    return lax.broadcasted_iota(jnp.int32, x.shape, 1)


def swap(x):
    return pltpu.roll(x, 64, 1)


def join(left, right):
    return jnp.where(lanes_of(left) < 64, left, right)


def put(half, side):
    return half if side == 0 else swap(half)


def one_hot(order, first, count):
    rows = lax.broadcasted_iota(jnp.int32, (count, order.shape[1]), 0) + first
    return jnp.where(rows == order, 1.0, 0.0)


def solve_kernel(
    rhs, order, linv, basis, cap,
    out,
    rhs_v, linv_v, basis_v, cap_v,
    uh, ul, wh, wl, uth, utl, fth, ftl, gram,
    hot, pick, xh, xl, gathered, oh, ol, field,
    qraw, q_in, q, y_in, za, z0, rr, x_in, c_in, z5s, z6s, dx, d_in, zt0, ztb,
    c1b, c3b, c5b, c6b, g_in, g0, g12, g1, g2r, g2, pk, pk_in, x4, z8, mx, mz,
    ssem, rsem, lsem,
):
    me = lax.axis_index("rows")
    core = lax.rem(me, 2)
    y = lax.rem(lax.div(me, 2), 4)
    x = lax.rem(lax.div(me, 8), 4)
    z = lax.div(me, 32)
    j = core * 4 + y
    plane = z * 32
    row = plane + x * 8
    cell = y * 2 + core

    y_members = [lax.rem(y + r, 4) for r in range(1, 4)]
    y_devices = [row + m * 2 + core for m in y_members]
    x_members = [lax.rem(x + r, 4) for r in range(1, 4)]
    x_devices = [plane + m * 8 + cell for m in x_members]
    z_members = [lax.rem(z + r, 8) for r in range(1, 8)]
    z_devices = [m * 32 + x * 8 + cell for m in z_members]
    other_core = row + y * 2 + (1 - core)

    def rows_at(index, count):
        return pl.ds(pl.multiple_of(index * count, count), count)

    used = [0]
    started = []

    def send(src, dst, device):
        at = used[0]
        used[0] += 1
        copy = pltpu.make_async_remote_copy(
            src_ref=src,
            dst_ref=dst,
            send_sem=ssem.at[at],
            recv_sem=rsem.at[at],
            device_id=(device,),
            device_id_type=MESH,
        )
        copy.start()
        started.append(copy)
        return copy

    def arrive(copies):
        for copy in copies:
            copy.wait_recv()

    def basis_load(c):
        rows = pl.ds(c * 256, 256)
        return pltpu.make_async_copy(basis.at[:, rows, :], basis_v.at[:, rows, :], lsem.at[c])

    def linv_load(c):
        rows = pl.ds(c * 512, 512)
        return pltpu.make_async_copy(linv.at[rows, :], linv_v.at[rows, :], lsem.at[8 + c])

    for c in range(4):
        basis_load(c).start()
    cap_load = pltpu.make_async_copy(cap, cap_v, lsem.at[16])
    cap_load.start()
    rhs_load = pltpu.make_async_copy(rhs, rhs_v, lsem.at[17])
    rhs_load.start()
    for c in range(2):
        linv_load(c).start()
    own = []
    for at, (level, buffer, node) in enumerate(
        ((1, c1b, lax.div(y, 2)), (3, c3b, lax.div(x, 2)), (5, c5b, lax.div(z, 2)), (6, c6b, lax.div(z, 4)))
    ):
        own.append(pltpu.make_async_copy(cap.at[level], buffer.at[node], lsem.at[18 + at]))
        own[-1].start()

    barrier = pltpu.get_barrier_semaphore()
    partners = [other_core] + y_devices + x_devices + z_devices
    for device in partners:
        pl.semaphore_signal(barrier, inc=1, device_id=(device,), device_id_type=MESH)

    def pack(c, carry):
        rows = rows_at(c, 256)
        basis_load(c).wait()
        for t in range(4):
            a = basis_v[PACKED[2 * t], rows, :]
            b = basis_v[PACKED[2 * t + 1], rows, :]
            u = join(a, swap(b))
            w = join(swap(a), b)
            cols = slice(128 * t, 128 * t + 128)
            uh[rows, cols], ul[rows, cols] = split(u)
            wh[rows, cols], wl[rows, cols] = split(w)
            uth[cols, rows], utl[cols, rows] = split(u.T)
        return carry

    lax.fori_loop(0, 4, pack, 0)

    pl.semaphore_wait(barrier, len(partners))
    cap_load.wait()
    for copy in own:
        copy.wait()
    c1_copies = [send(cap_v.at[1], c1b.at[lax.div(y, 2)], y_devices[1])]

    g_copies = []
    for t, low in ((0, 0), (3, 0), (1, 128), (2, 256)):
        rows = slice(128 * t, 128 * t + 128)
        gram[rows, low:] = dot3((uth[rows, :], utl[rows, :]), (wh[:, low:], wl[:, low:]))
        if t == 3:
            g0[rows_at(core, 64), :] = gram[448:512, :]
            g0_copies = [send(gram.at[pl.ds(448, 64), :], g0.at[rows_at(core, 64), :], other_core)]
        else:
            at = gram.at[pl.ds(128 * t, 128), pl.ds(low, 512 - low)]
            to = g_in.at[pl.ds(128 * t, 128), pl.ds(low, 512 - low)]
            g_copies.append(send(at, to, other_core))
    c3_copies = [send(cap_v.at[3], c3b.at[lax.div(x, 2)], x_devices[1])]
    c5_copies = [send(cap_v.at[5], c5b.at[lax.div(z, 2)], z_devices[r - 1]) for r in (2, 4, 6)]
    c6_copies = [send(cap_v.at[6], c6b.at[lax.div(z, 4)], z_devices[3])]

    rhs_load.wait()
    local = order[...] - me * 512
    for b in range(4):
        block = one_hot(local, 128 * b, 128)
        hot[128 * b : 128 * b + 128, :] = block.astype(BF16)
        pick[:, 128 * b : 128 * b + 128] = block.T.astype(BF16)
    for c in range(2):
        for half in range(2):
            cols = slice((2 * c + half) * 128, (2 * c + half) * 128 + 128)
            xh[:, cols], xl[:, cols] = split(rhs_v[pl.ds(2 * half + c, 512, stride=4), :])

    arrive(g_copies[:1])
    for level in range(2):
        rows = pl.ds(pl.multiple_of(64 * level + 32 * core, 32), 32)
        tiles = [gram[rows, low : low + 128] + g_in[rows, low : low + 128] for low in (0, 128, 256, 384)]
        g12[level, :, 0:128] = join(tiles[3], tiles[0])
        g12[level, :, 128:256] = tiles[1]
        g12[level, :, 256:384] = tiles[2]
    core_rows = rows_at(core, 32)
    g1[y, core_rows, :] = g12[0]
    g2r[y, :, :] = g12[1]
    g1_copies = [send(g12.at[0], g1.at[y, core_rows, :], d) for d in y_devices]
    g2_copies = [send(g12.at[1], g2r.at[y], d) for d in y_devices]

    for source, target in ((xh, oh), (xl, ol)):
        for b in range(4):
            moved = mm(pick[128 * b : 128 * b + 128, :], source[...])
            for c in range(2):
                for half in range(2):
                    at = (2 * c + half) * 128
                    gathered[half, pl.ds(256 * b + c, 128, stride=2), :] = moved[:, at : at + 128]
        for half in range(2):
            target[:, 128 * half : 128 * half + 128] = gathered[half].astype(BF16)

    arrive(g_copies[1:])
    for at, base in ((0, 128), (256, 192)):
        rows = slice(base, base + 64)
        tiles = [gram[rows, low : low + 128] + g_in[rows, low : low + 128] for low in (128, 256, 384)]
        pk[:, at : at + 128] = join(tiles[2], tiles[0])
        pk[:, at + 128 : at + 256] = tiles[1]
    for at, base in ((512, 256), (640, 320)):
        rows = slice(base, base + 64)
        tiles = [gram[rows, low : low + 128] + g_in[rows, low : low + 128] for low in (256, 384)]
        pk[:, at : at + 128] = join(tiles[1], tiles[0])
    pk_in[y] = pk[rows_at(j, 8), :]
    pk_copies = [
        send(pk.at[rows_at(core * 4 + m, 8), :], pk_in.at[y], d) for m, d in zip(y_members, y_devices)
    ]

    def leaf(c, carry):
        rows = rows_at(c, 512)
        linv_load(c).wait()
        value = dot3(split(linv_v[rows, :]), (oh[...], ol[...]))
        field[0, rows, :] = value[:, :128]
        field[1, rows, :] = value[:, 128:]
        fth[:, rows], ftl[:, rows] = split(value.T)
        return carry

    lax.fori_loop(0, 2, leaf, 0)
    qraw[...] = dot3((fth[...], ftl[...]), (wh[...], wl[...]))

    own_half = rows_at(core, 128)
    q_copies = [send(qraw.at[rows_at(1 - core, 128), :], q_in, other_core)]
    own_rows = rows_at(j, 8)
    arrive(pk_copies)
    x4[x] = pk_in[0] + pk_in[1] + pk_in[2] + pk_in[3]
    x4_copies = [send(x4.at[x], x4.at[x], d) for d in x_devices]
    arrive(g0_copies)
    arrive(q_copies)
    mine, others = qraw[own_half, :], q_in[...]
    first = jnp.where(core == 0, mine[:, 384:], others[:, 384:])
    second = jnp.where(core == 0, others[:, 384:], mine[:, 384:])
    solved = product(join(swap(second), first), cap_v[0], True)
    q[...] = mine + others - product(solved, g0[...])

    y_in[y] = q[rows_at(y, 32), :]
    y_copies = [send(q.at[rows_at(m, 32), :], y_in.at[y], d) for m, d in zip(y_members, y_devices)]
    swapped = swap(solved)
    z0[0] = solved
    z0[1] = swapped
    z0_copies = [send(z0.at[core], z0.at[2], other_core)]
    arrive(g1_copies)
    arrive(g2_copies)
    g2[0, core_rows, :] = g2r[0] + g2r[1]
    g2[1, core_rows, :] = g2r[2] + g2r[3]
    g12c_copies = [
        send(g1.at[:, core_rows, :], g1.at[:, core_rows, :], other_core),
        send(g2.at[:, core_rows, :], g2.at[:, core_rows, :], other_core),
    ]
    arrive(x4_copies)
    for m in range(4):
        mx[m, own_rows, :] = x4[m, :, 0:256]
    for h in range(2):
        mx[4 + h, own_rows, :] = x4[2 * h, :, 256:512] + x4[2 * h + 1, :, 256:512]
    z8[z] = x4[0, :, 512:] + x4[1, :, 512:] + x4[2, :, 512:] + x4[3, :, 512:]
    z8_copies = [send(z8.at[z], z8.at[z], d) for d in z_devices]
    arrive(c1_copies)
    arrive(g12c_copies)
    m1 = [jnp.concatenate([g1[2 * n], g1[2 * n + 1]], 0) for n in range(2)]
    m2 = jnp.concatenate([g2[0], g2[1]], 0)
    arrive(y_copies)
    mxy_copies = [send(mx.at[:, own_rows, :], mx.at[:, own_rows, :], d) for d in y_devices]
    low = [y_in[m, :, 0:128] for m in range(4)]
    z1 = [product(join(low[2 * n + 1], swap(low[2 * n])), c1b[n], True) for n in range(2)]
    y1 = [product(z1[n], m1[n]) for n in range(2)]
    left = [low[2 * h] + low[2 * h + 1] - y1[h][:, :128] for h in range(2)]
    z2 = product(join(swap(left[1]), left[0]), cap_v[2], True)
    taken = y1[0] + y1[1] + product(z2, m2)
    high = y_in[0, :, 128:] + y_in[1, :, 128:] + y_in[2, :, 128:] + y_in[3, :, 128:]
    rr[:, 0:256] = high[:, 0:256] - taken[:, 128:]
    rr[:, 256:384] = high[:, 256:] - taken[:, :128]

    x_in[x] = rr[rows_at(x, 8), :]
    x_copies = [send(rr.at[rows_at(m, 8), :], x_in.at[x], d) for m, d in zip(x_members, x_devices)]
    for m in range(4):
        za[m] = join(put(z1[m // 2], m % 2), put(z2, 1 - m // 2))
    own_cols = rows_at(j, 32)
    zt0[own_cols, :] = za[y]
    za_copies = [send(za.at[m], zt0.at[own_cols, :], d) for m, d in zip(y_members, y_devices)]
    arrive(z8_copies)
    for m in range(8):
        mz[m, own_rows, :] = z8[m, :, 0:128]
    for p in range(4):
        mz[8 + p, own_rows, :] = z8[2 * p, :, 128:] + z8[2 * p + 1, :, 128:]
    mzy_copies = [send(mz.at[:, own_rows, :], mz.at[:, own_rows, :], d) for d in y_devices]
    arrive(c3_copies)
    arrive(mxy_copies)
    mxc_copies = [send(mx.at[:, core_rows, :], mx.at[:, core_rows, :], other_core)]
    arrive(mxc_copies)
    m3 = [jnp.concatenate([mx[2 * n], mx[2 * n + 1]], 0) for n in range(2)]
    m4 = jnp.concatenate([mx[4], mx[5]], 0)
    arrive(x_copies)
    low = [x_in[m, :, 0:128] for m in range(4)]
    z3 = [product(join(low[2 * n + 1], swap(low[2 * n])), c3b[n], True) for n in range(2)]
    y3 = [product(z3[n], m3[n]) for n in range(2)]
    left = [low[2 * h] + low[2 * h + 1] - y3[h][:, :128] for h in range(2)]
    z4 = product(join(swap(left[1]), left[0]), cap_v[4], True)
    taken = y3[0] + y3[1] + product(z4, m4)
    high = x_in[0, :, 128:] + x_in[1, :, 128:] + x_in[2, :, 128:] + x_in[3, :, 128:]
    high = jnp.concatenate([high[:, :128] - taken[:, 128:], high[:, 128:] - taken[:, :128]], 1)

    c_in[z] = high
    c_copies = [send(c_in.at[z], c_in.at[z], d) for d in z_devices]
    for m in range(4):
        dx[m, :, 0:128] = join(put(z3[m // 2], m % 2), put(z4, 1 - m // 2))
    arrive(mzy_copies)
    mzc_copies = [send(mz.at[:, core_rows, :], mz.at[:, core_rows, :], other_core)]
    arrive(za_copies)
    half_cols = rows_at(core, 128)
    zac_copies = [send(zt0.at[half_cols, :], zt0.at[half_cols, :], other_core)]
    arrive(c5_copies)
    arrive(c6_copies)
    arrive(mzc_copies)
    m5 = [jnp.concatenate([mz[2 * p], mz[2 * p + 1]], 0) for p in range(4)]
    m6 = [jnp.concatenate([mz[8 + 2 * n], mz[9 + 2 * n]], 0) for n in range(2)]
    arrive(c_copies)
    low = [c_in[m, :, 0:128] for m in range(8)]
    top = [c_in[m, :, 128:] for m in range(8)]
    z5 = [product(join(low[2 * p + 1], swap(low[2 * p])), c5b[p], True) for p in range(4)]
    y5 = [product(z5[p], m5[p]) for p in range(4)]
    left = [low[2 * p] + low[2 * p + 1] - y5[p] for p in range(4)]
    z6 = [product(join(swap(left[2 * n + 1]), left[2 * n]), c6b[n], True) for n in range(2)]
    y6 = [product(z6[n], m6[n]) for n in range(2)]
    left = []
    for h in range(2):
        value = top[4 * h] + top[4 * h + 1] + top[4 * h + 2] + top[4 * h + 3]
        left.append(value - y5[2 * h] - y5[2 * h + 1] - y6[h])
    z7 = product(join(left[1], swap(left[0])), cap_v[7], True)
    for p in range(4):
        z5s[p] = z5[p]
    for n in range(2):
        z6s[n] = z6[n]
    side5, side6, side7 = lax.rem(z, 2), lax.rem(lax.div(z, 2), 2), lax.div(z, 4)
    own5 = z5s[lax.div(z, 2)]
    own5 = jnp.where(side5 == 0, own5, swap(own5))
    own6 = z6s[lax.div(z, 4)]
    own6 = jnp.where(side6 == 0, swap(own6), own6)
    own7 = jnp.where(side7 == 0, z7, swap(z7))
    middle = join(own5, own6)
    for m in range(4):
        dx[m, :, 128:256] = middle
        dx[m, :, 256:384] = own7

    x_rows = rows_at(x, 8)
    d_in[x_rows, :] = dx[x]
    d_copies = [send(dx.at[m], d_in.at[x_rows, :], d) for m, d in zip(x_members, x_devices)]
    arrive(d_copies)
    ztb[own_cols, :] = d_in[...]
    ztb_copies = [send(d_in, ztb.at[own_cols, :], d) for d in y_devices]
    arrive(ztb_copies)
    ztbc_copies = [send(ztb.at[half_cols, :], ztb.at[half_cols, :], other_core)]
    arrive(z0_copies)
    arrive(zac_copies)
    arrive(ztbc_copies)
    near = z0[1 - core]
    far = z0[2]
    own0 = jnp.concatenate([jnp.where(core == 0, near, far), jnp.where(core == 0, far, near)], 0)
    whole = jnp.concatenate([zt0[...], ztb[:, 0:256], join(ztb[:, 256:], own0)], 1).T
    xh[:, 0:256], xl[:, 0:256] = split(whole)

    def update(c, carry):
        rows = rows_at(c, 512)
        taken = dot3((uh[rows, :], ul[rows, :]), (xh[:, 0:256], xl[:, 0:256]))
        field[0, rows, :] = field[0, rows, :] - taken[:, :128]
        field[1, rows, :] = field[1, rows, :] - taken[:, 128:]
        return carry

    lax.fori_loop(0, 2, update, 0)

    for c in range(2):
        value = jnp.concatenate([field[h, pl.ds(c, 512, stride=2), :] for h in range(2)], 1)
        xh[:, 256 * c : 256 * c + 256], xl[:, 256 * c : 256 * c + 256] = split(value)
    for b in range(4):
        rows = slice(128 * b, 128 * b + 128)
        moved = mm(hot[rows, :], xh[...]) + mm(hot[rows, :], xl[...])
        for c in range(2):
            for h in range(2):
                at = 256 * c + 128 * h
                out[pl.ds(512 * b + 2 * h + c, 128, stride=4), :] = moved[:, at : at + 128]
    for copy in started:
        copy.wait_send()
    assert used[0] == COPIES


def shards(right_sides, order, leaf_inverse, basis, capacitance):
    rhs = right_sides.reshape(512, 2, 2, 128).transpose(0, 2, 1, 3).reshape(2048, 128)
    order = order.reshape(1, 512)
    any_ref = pl.BlockSpec(memory_space=pl.ANY)
    vmem_ref = pl.BlockSpec(memory_space=pltpu.VMEM)
    f, h = (lambda *shape: pltpu.VMEM(shape, F32)), (lambda *shape: pltpu.VMEM(shape, BF16))
    out = pl.pallas_call(
        solve_kernel,
        out_shape=jax.ShapeDtypeStruct((2048, 128), F32),
        in_specs=[any_ref, vmem_ref, any_ref, any_ref, any_ref],
        out_specs=vmem_ref,
        scratch_shapes=[
            f(2048, 128), f(1024, 1024), f(8, 1024, 128), f(8, 128, 128),
            h(1024, 512), h(1024, 512), h(1024, 512), h(1024, 512),
            h(512, 1024), h(512, 1024), h(256, 1024), h(256, 1024), f(512, 512),
            h(512, 512), h(512, 512), h(512, 512), h(512, 512), f(2, 1024, 128),
            h(1024, 256), h(1024, 256), f(2, 1024, 128),
            f(256, 512), f(128, 512), f(128, 512), f(4, 32, 512), f(4, 32, 128), f(3, 128, 128),
            f(32, 384), f(4, 8, 384), f(8, 8, 256), f(4, 8, 128), f(2, 8, 128), f(4, 8, 384),
            f(32, 384), f(256, 128), f(256, 384),
            f(2, 128, 128), f(2, 128, 128), f(4, 128, 128), f(2, 128, 128),
            f(512, 512), f(128, 512), f(2, 32, 384), f(4, 64, 384), f(4, 32, 384), f(2, 64, 384),
            f(64, 768), f(4, 8, 768), f(4, 8, 768), f(8, 8, 256), f(6, 64, 256), f(12, 64, 128),
            pltpu.SemaphoreType.DMA((COPIES,)), pltpu.SemaphoreType.DMA((COPIES,)),
            pltpu.SemaphoreType.DMA((22,)),
        ],
        compiler_params=pltpu.CompilerParams(
            collective_id=0, has_side_effects=True, vmem_limit_bytes=VMEM_BYTES
        ),
    )(rhs, order, leaf_inverse, basis, capacitance.reshape(8, 128, 128))
    return out.reshape(512, 2, 2, 128).transpose(0, 2, 1, 3).reshape(512, 2, 256)


def solution(mesh):
    return jax.shard_map(
        shards,
        mesh=mesh,
        in_specs=(
            P("rows", None, None),
            P("rows"),
            P("rows", None),
            P(None, "rows", None),
            P(None, "rows", None, None),
        ),
        out_specs=P("rows", None, None),
        check_vma=False,
    )
```

time: 69 us -> 56.7 us (0.82)
  Pallas kernels: 67.6 us -> 54 us
  local copies, waits for them, and re-layouts: 1.22 us -> 2.55 us
    pallas_call x2 -> x1, Pallas kernels: 67.6 us -> 54 us  [shards(): pl.pallas_call(solve_kernel, out_shape=jax.ShapeDtypeStruct((2048, 128),...]
    unnamed x4 -> x1, local copies, waits for them, and re-layouts: 1.22 us -> 2.55 us
where the time goes in v2:
time: 56.7 us; the launch traced here: 56.6 us
  Pallas kernels  54 us (95%)
  local copies, waits for them, and re-layouts  2.55 us (4%)
    pallas_call x1, Pallas kernels, shards(): pl.pallas_call(solve_kernel, out_shape=jax.ShapeDtypeStruct((2048, 128),...  54 us
    unnamed x1, local copies, waits for them, and re-layouts  2.55 us

profile of v2, /device:TPU:1, one launch (start us, length us, event | category | flops | bytes accessed | tf_op | source)
XLA Modules:
  0.0 56.6 jit_solution(16245296649275572826)
XLA Ops:
  0.0 54.0 %shard_map.55 = f32[2048,128]{1,0:T(8,128)} custom-call(f32[2048,128]{1,0:T(8,128)} %bitcast.13, s32[1,512]{1,0:T(1,128)} %bitcast.15, f32[1024,1024]{1,0:T(8,128)} %linv.1, f32[8,1024,128]{2,1,0:T(8,128)} %basis.1, f32[8,128,128]{2,1,0:T(8,128)} %bitcast.14), custom_call_target="tpu_custom_call" | custom-call | tf_op jit(solution)/shard_map/pallas_call | solution.py:408
  54.0 2.6 %copy.9 = f32[512,2,256]{2,1,0:T(2,128)} copy(f32[512,2,256]{2,1,0:T(2,128)} %bitcast.12) | data formatting | bytes 2097152

commit v3 on v2

--- a/solution.py
+++ b/solution.py
@@ -11,8 +11,8 @@
 BF16 = jnp.bfloat16
 MESH = pl.DeviceIdType.MESH
 PACKED = (1, 2, 3, 4, 5, 6, 7, 0)
-COPIES = 65
-VMEM_BYTES = 56 * 1024 * 1024
+COPIES = 75
+VMEM_BYTES = 58 * 1024 * 1024
 
 
 def split(x):
@@ -59,10 +59,10 @@
 
 def solve_kernel(
     rhs, order, linv, basis, cap,
-    out,
+    field,
     rhs_v, linv_v, basis_v, cap_v,
     uh, ul, wh, wl, uth, utl, fth, ftl, gram,
-    hot, pick, xh, xl, gathered, oh, ol, field,
+    pick, xh, xl, gathered, oh, ol,
     qraw, q_in, q, y_in, za, z0, rr, x_in, c_in, z5s, z6s, dx, d_in, zt0, ztb,
     c1b, c3b, c5b, c6b, g_in, g0, g12, g1, g2r, g2, pk, pk_in, x4, z8, mx, mz,
     ssem, rsem, lsem,
@@ -126,12 +126,6 @@
     rhs_load.start()
     for c in range(2):
         linv_load(c).start()
-    own = []
-    for at, (level, buffer, node) in enumerate(
-        ((1, c1b, lax.div(y, 2)), (3, c3b, lax.div(x, 2)), (5, c5b, lax.div(z, 2)), (6, c6b, lax.div(z, 4)))
-    ):
-        own.append(pltpu.make_async_copy(cap.at[level], buffer.at[node], lsem.at[18 + at]))
-        own[-1].start()
 
     barrier = pltpu.get_barrier_semaphore()
     partners = [other_core] + y_devices + x_devices + z_devices
@@ -154,16 +148,12 @@
 
     lax.fori_loop(0, 4, pack, 0)
 
-    pl.semaphore_wait(barrier, len(partners))
-    cap_load.wait()
-    for copy in own:
-        copy.wait()
-    c1_copies = [send(cap_v.at[1], c1b.at[lax.div(y, 2)], y_devices[1])]
-
     g_copies = []
     for t, low in ((0, 0), (3, 0), (1, 128), (2, 256)):
         rows = slice(128 * t, 128 * t + 128)
         gram[rows, low:] = dot3((uth[rows, :], utl[rows, :]), (wh[:, low:], wl[:, low:]))
+        if t == 0:
+            pl.semaphore_wait(barrier, len(partners))
         if t == 3:
             g0[rows_at(core, 64), :] = gram[448:512, :]
             g0_copies = [send(gram.at[pl.ds(448, 64), :], g0.at[rows_at(core, 64), :], other_core)]
@@ -171,16 +161,23 @@
             at = gram.at[pl.ds(128 * t, 128), pl.ds(low, 512 - low)]
             to = g_in.at[pl.ds(128 * t, 128), pl.ds(low, 512 - low)]
             g_copies.append(send(at, to, other_core))
-    c3_copies = [send(cap_v.at[3], c3b.at[lax.div(x, 2)], x_devices[1])]
-    c5_copies = [send(cap_v.at[5], c5b.at[lax.div(z, 2)], z_devices[r - 1]) for r in (2, 4, 6)]
-    c6_copies = [send(cap_v.at[6], c6b.at[lax.div(z, 4)], z_devices[3])]
+    cap_load.wait()
+    halves, eighths = rows_at(core, 64), rows_at(j, 16)
+    c1b[lax.div(y, 2)] = cap_v[1]
+    c3b[lax.div(x, 2)] = cap_v[3]
+    c5b[lax.div(z, 2), eighths, :] = cap_v[5, eighths, :]
+    c6b[lax.div(z, 4), eighths, :] = cap_v[6, eighths, :]
+    c1_copies = [send(cap_v.at[1, halves, :], c1b.at[lax.div(y, 2), halves, :], y_devices[1])]
+    c3_copies = [send(cap_v.at[3, halves, :], c3b.at[lax.div(x, 2), halves, :], x_devices[1])]
+    c5_copies = [
+        send(cap_v.at[5, eighths, :], c5b.at[lax.div(z, 2), eighths, :], z_devices[r - 1]) for r in (2, 4, 6)
+    ]
+    c6_copies = [send(cap_v.at[6, eighths, :], c6b.at[lax.div(z, 4), eighths, :], z_devices[3])]
 
     rhs_load.wait()
     local = order[...] - me * 512
     for b in range(4):
-        block = one_hot(local, 128 * b, 128)
-        hot[128 * b : 128 * b + 128, :] = block.astype(BF16)
-        pick[:, 128 * b : 128 * b + 128] = block.T.astype(BF16)
+        pick[:, 128 * b : 128 * b + 128] = one_hot(local, 128 * b, 128).T.astype(BF16)
     for c in range(2):
         for half in range(2):
             cols = slice((2 * c + half) * 128, (2 * c + half) * 128 + 128)
@@ -260,7 +257,10 @@
     arrive(g2_copies)
     g2[0, core_rows, :] = g2r[0] + g2r[1]
     g2[1, core_rows, :] = g2r[2] + g2r[3]
+    arrive(c1_copies)
+    far1 = 1 - lax.div(y, 2)
     g12c_copies = [
+        send(c1b.at[far1, halves, :], c1b.at[far1, halves, :], other_core),
         send(g1.at[:, core_rows, :], g1.at[:, core_rows, :], other_core),
         send(g2.at[:, core_rows, :], g2.at[:, core_rows, :], other_core),
     ]
@@ -271,7 +271,6 @@
         mx[4 + h, own_rows, :] = x4[2 * h, :, 256:512] + x4[2 * h + 1, :, 256:512]
     z8[z] = x4[0, :, 512:] + x4[1, :, 512:] + x4[2, :, 512:] + x4[3, :, 512:]
     z8_copies = [send(z8.at[z], z8.at[z], d) for d in z_devices]
-    arrive(c1_copies)
     arrive(g12c_copies)
     m1 = [jnp.concatenate([g1[2 * n], g1[2 * n + 1]], 0) for n in range(2)]
     m2 = jnp.concatenate([g2[0], g2[1]], 0)
@@ -300,9 +299,17 @@
     for p in range(4):
         mz[8 + p, own_rows, :] = z8[2 * p, :, 128:] + z8[2 * p + 1, :, 128:]
     mzy_copies = [send(mz.at[:, own_rows, :], mz.at[:, own_rows, :], d) for d in y_devices]
+    arrive(c5_copies)
+    arrive(c6_copies)
+    mzy_copies += [send(c5b.at[:, eighths, :], c5b.at[:, eighths, :], d) for d in y_devices]
+    mzy_copies += [send(c6b.at[:, eighths, :], c6b.at[:, eighths, :], d) for d in y_devices]
     arrive(c3_copies)
     arrive(mxy_copies)
-    mxc_copies = [send(mx.at[:, core_rows, :], mx.at[:, core_rows, :], other_core)]
+    far3 = 1 - lax.div(x, 2)
+    mxc_copies = [
+        send(mx.at[:, core_rows, :], mx.at[:, core_rows, :], other_core),
+        send(c3b.at[far3, halves, :], c3b.at[far3, halves, :], other_core),
+    ]
     arrive(mxc_copies)
     m3 = [jnp.concatenate([mx[2 * n], mx[2 * n + 1]], 0) for n in range(2)]
     m4 = jnp.concatenate([mx[4], mx[5]], 0)
@@ -321,12 +328,14 @@
     for m in range(4):
         dx[m, :, 0:128] = join(put(z3[m // 2], m % 2), put(z4, 1 - m // 2))
     arrive(mzy_copies)
-    mzc_copies = [send(mz.at[:, core_rows, :], mz.at[:, core_rows, :], other_core)]
+    mzc_copies = [
+        send(mz.at[:, core_rows, :], mz.at[:, core_rows, :], other_core),
+        send(c5b.at[:, halves, :], c5b.at[:, halves, :], other_core),
+        send(c6b.at[:, halves, :], c6b.at[:, halves, :], other_core),
+    ]
     arrive(za_copies)
     half_cols = rows_at(core, 128)
     zac_copies = [send(zt0.at[half_cols, :], zt0.at[half_cols, :], other_core)]
-    arrive(c5_copies)
-    arrive(c6_copies)
     arrive(mzc_copies)
     m5 = [jnp.concatenate([mz[2 * p], mz[2 * p + 1]], 0) for p in range(4)]
     m6 = [jnp.concatenate([mz[8 + 2 * n], mz[9 + 2 * n]], 0) for n in range(2)]
@@ -383,20 +392,29 @@
         return carry
 
     lax.fori_loop(0, 2, update, 0)
-
+    for copy in started:
+        copy.wait_send()
+    assert used[0] == COPIES
+
+
+def scatter_kernel(field, order, out, high, low, done, sems):
+    local = order[...] - lax.axis_index("rows") * 512
     for c in range(2):
         value = jnp.concatenate([field[h, pl.ds(c, 512, stride=2), :] for h in range(2)], 1)
-        xh[:, 256 * c : 256 * c + 256], xl[:, 256 * c : 256 * c + 256] = split(value)
+        high[:, 256 * c : 256 * c + 256], low[:, 256 * c : 256 * c + 256] = split(value)
+    copies = []
     for b in range(4):
-        rows = slice(128 * b, 128 * b + 128)
-        moved = mm(hot[rows, :], xh[...]) + mm(hot[rows, :], xl[...])
+        pick = one_hot(local, 128 * b, 128).astype(BF16)
+        moved = mm(pick, high[...]) + mm(pick, low[...])
         for c in range(2):
             for h in range(2):
                 at = 256 * c + 128 * h
-                out[pl.ds(512 * b + 2 * h + c, 128, stride=4), :] = moved[:, at : at + 128]
-    for copy in started:
-        copy.wait_send()
-    assert used[0] == COPIES
+                done[pl.ds(512 * b + 2 * h + c, 128, stride=4), :] = moved[:, at : at + 128]
+        rows = pl.ds(512 * b, 512)
+        copies.append(pltpu.make_async_copy(done.at[rows, :], out.at[rows, :], sems.at[b]))
+        copies[-1].start()
+    for copy in copies:
+        copy.wait()
 
 
 def shards(right_sides, order, leaf_inverse, basis, capacitance):
@@ -405,17 +423,17 @@
     any_ref = pl.BlockSpec(memory_space=pl.ANY)
     vmem_ref = pl.BlockSpec(memory_space=pltpu.VMEM)
     f, h = (lambda *shape: pltpu.VMEM(shape, F32)), (lambda *shape: pltpu.VMEM(shape, BF16))
-    out = pl.pallas_call(
+    field = pl.pallas_call(
         solve_kernel,
-        out_shape=jax.ShapeDtypeStruct((2048, 128), F32),
+        out_shape=pltpu.VMEM((2, 1024, 128), F32),
         in_specs=[any_ref, vmem_ref, any_ref, any_ref, any_ref],
         out_specs=vmem_ref,
         scratch_shapes=[
             f(2048, 128), f(1024, 1024), f(8, 1024, 128), f(8, 128, 128),
             h(1024, 512), h(1024, 512), h(1024, 512), h(1024, 512),
             h(512, 1024), h(512, 1024), h(256, 1024), h(256, 1024), f(512, 512),
-            h(512, 512), h(512, 512), h(512, 512), h(512, 512), f(2, 1024, 128),
-            h(1024, 256), h(1024, 256), f(2, 1024, 128),
+            h(512, 512), h(512, 512), h(512, 512), f(2, 1024, 128),
+            h(1024, 256), h(1024, 256),
             f(256, 512), f(128, 512), f(128, 512), f(4, 32, 512), f(4, 32, 128), f(3, 128, 128),
             f(32, 384), f(4, 8, 384), f(8, 8, 256), f(4, 8, 128), f(2, 8, 128), f(4, 8, 384),
             f(32, 384), f(256, 128), f(256, 384),
@@ -429,6 +447,14 @@
             collective_id=0, has_side_effects=True, vmem_limit_bytes=VMEM_BYTES
         ),
     )(rhs, order, leaf_inverse, basis, capacitance.reshape(8, 128, 128))
+    out = pl.pallas_call(
+        scatter_kernel,
+        out_shape=jax.ShapeDtypeStruct((2048, 128), F32),
+        in_specs=[vmem_ref, vmem_ref],
+        out_specs=any_ref,
+        scratch_shapes=[h(512, 512), h(512, 512), f(2048, 128), pltpu.SemaphoreType.DMA((4,))],
+        compiler_params=pltpu.CompilerParams(vmem_limit_bytes=16 * 1024 * 1024),
+    )(field, order)
     return out.reshape(512, 2, 2, 128).transpose(0, 2, 1, 3).reshape(512, 2, 256)
 
 

time: 56.7 us -> 54.7 us (0.965)
  local copies, waits for them, and re-layouts: 2.55 us -> 0.01 us
  Pallas kernels: 54 us -> 54.6 us
    unnamed x1 -> x2, local copies, waits for them, and re-layouts: 2.55 us -> 0.01 us
    pallas_call x1 -> x2, Pallas kernels: 54 us -> 54.6 us  [the longest x1 53.1 us: shards(): pl.pallas_call(solve_kernel, out_shape=pltpu.VMEM((2, 1024, 128), F32), i...]
where the time goes in v3:
time: 54.7 us; the launch traced here: 54.6 us
  Pallas kernels  54.6 us (100%)
    pallas_call x1, Pallas kernels, shards(): pl.pallas_call(solve_kernel, out_shape=pltpu.VMEM((2, 1024, 128), F32), i...  53.1 us
    pallas_call x1, Pallas kernels, shards(): pl.pallas_call(scatter_kernel, out_shape=jax.ShapeDtypeStruct((2048, 128)...  1.5 us

profile of v3, /device:TPU:1, one launch (start us, length us, event | category | flops | bytes accessed | tf_op | source)
XLA Modules:
  0.0 54.6 jit_solution(18373403120196579733)
XLA Ops:
  0.0 0.0 copy-start
  0.0 53.1 %shard_map.55.field = f32[2,1024,128]{2,1,0:T(8,128)S(1)} custom-call(f32[2048,128]{1,0:T(8,128)} %bitcast.14, s32[1,512]{1,0:T(1,128)} %bitcast.12, f32[1024,1024]{1,0:T(8,128)} %linv.1, f32[8,1024,128]{2,1,0:T(8,128)} %basis.1, f32[8,128,128]{2,1,0:T(8,128)} %bitcast.15), custom_call_target="tpu_custom_call" | custom-call | tf_op jit(solution)/shard_map/pallas_call | solution.py:426
  53.1 0.0 copy-done
  53.1 1.5 %shard_map.56 = f32[2048,128]{1,0:T(8,128)} custom-call(f32[2,1024,128]{2,1,0:T(8,128)S(1)} %shard_map.55.field, s32[1,512]{1,0:T(1,128)S(1)} %bitcast.13), custom_call_target="tpu_custom_call" | custom-call | tf_op jit(solution)/shard_map/pallas_call | solution.py:450
Async XLA Ops:
  0.0 53.1 %copy-start = (s32[512]{0:T(512)S(1)}, s32[512]{0:T(512)}, u32[]{:S(2)}) copy-start(s32[512]{0:T(512)} %param.6) | copy-start | bytes 6148

commit v4 on v3

--- a/solution.py
+++ b/solution.py
@@ -11,7 +11,7 @@
 BF16 = jnp.bfloat16
 MESH = pl.DeviceIdType.MESH
 PACKED = (1, 2, 3, 4, 5, 6, 7, 0)
-COPIES = 75
+COPIES = 100
 VMEM_BYTES = 58 * 1024 * 1024
 
 
@@ -63,7 +63,7 @@
     rhs_v, linv_v, basis_v, cap_v,
     uh, ul, wh, wl, uth, utl, fth, ftl, gram,
     pick, xh, xl, gathered, oh, ol,
-    qraw, q_in, q, y_in, za, z0, rr, x_in, c_in, z5s, z6s, dx, d_in, zt0, ztb,
+    qraw, q_in, q, y_in, za, z0, rr, x_in, c_in, z5s, z6s, dx, d_out, zt0, zt1, ztb,
     c1b, c3b, c5b, c6b, g_in, g0, g12, g1, g2r, g2, pk, pk_in, x4, z8, mx, mz,
     ssem, rsem, lsem,
 ):
@@ -84,6 +84,10 @@
     z_members = [lax.rem(z + r, 8) for r in range(1, 8)]
     z_devices = [m * 32 + x * 8 + cell for m in z_members]
     other_core = row + y * 2 + (1 - core)
+    plane_members = []
+    for dy, dx_ in ((2, 2), (2, 1), (2, 3), (1, 2), (3, 2), (1, 1), (1, 3), (3, 1), (3, 3), (2, 0), (0, 2), (1, 0), (3, 0), (0, 1), (0, 3)):
+        other_y, other_x = lax.rem(y + dy, 4), lax.rem(x + dx_, 4)
+        plane_members.append((other_x, plane + other_x * 8 + other_y * 2 + core))
 
     def rows_at(index, count):
         return pl.ds(pl.multiple_of(index * count, count), count)
@@ -128,7 +132,7 @@
         linv_load(c).start()
 
     barrier = pltpu.get_barrier_semaphore()
-    partners = [other_core] + y_devices + x_devices + z_devices
+    partners = [other_core] + [d for _, d in plane_members] + z_devices
     for device in partners:
         pl.semaphore_signal(barrier, inc=1, device_id=(device,), device_id_type=MESH)
 
@@ -196,16 +200,6 @@
     g1_copies = [send(g12.at[0], g1.at[y, core_rows, :], d) for d in y_devices]
     g2_copies = [send(g12.at[1], g2r.at[y], d) for d in y_devices]
 
-    for source, target in ((xh, oh), (xl, ol)):
-        for b in range(4):
-            moved = mm(pick[128 * b : 128 * b + 128, :], source[...])
-            for c in range(2):
-                for half in range(2):
-                    at = (2 * c + half) * 128
-                    gathered[half, pl.ds(256 * b + c, 128, stride=2), :] = moved[:, at : at + 128]
-        for half in range(2):
-            target[:, 128 * half : 128 * half + 128] = gathered[half].astype(BF16)
-
     arrive(g_copies[1:])
     for at, base in ((0, 128), (256, 192)):
         rows = slice(base, base + 64)
@@ -221,6 +215,16 @@
         send(pk.at[rows_at(core * 4 + m, 8), :], pk_in.at[y], d) for m, d in zip(y_members, y_devices)
     ]
 
+    for source, target in ((xh, oh), (xl, ol)):
+        for b in range(4):
+            moved = mm(pick[128 * b : 128 * b + 128, :], source[...])
+            for c in range(2):
+                for half in range(2):
+                    at = (2 * c + half) * 128
+                    gathered[half, pl.ds(256 * b + c, 128, stride=2), :] = moved[:, at : at + 128]
+        for half in range(2):
+            target[:, 128 * half : 128 * half + 128] = gathered[half].astype(BF16)
+
     def leaf(c, carry):
         rows = rows_at(c, 512)
         linv_load(c).wait()
@@ -232,6 +236,19 @@
 
     lax.fori_loop(0, 2, leaf, 0)
     qraw[...] = dot3((fth[...], ftl[...]), (wh[...], wl[...]))
+
+    def update(cols, value):
+        width = value.shape[1]
+        xh[0:width, 0:256], xl[0:width, 0:256] = split(value.T)
+
+        def step(c, carry):
+            rows = rows_at(c, 512)
+            taken = dot3((uh[rows, cols], ul[rows, cols]), (xh[0:width, 0:256], xl[0:width, 0:256]))
+            field[0, rows, :] = field[0, rows, :] - taken[:, :128]
+            field[1, rows, :] = field[1, rows, :] - taken[:, 128:]
+            return carry
+
+        lax.fori_loop(0, 2, step, 0)
 
     own_half = rows_at(core, 128)
     q_copies = [send(qraw.at[rows_at(1 - core, 128), :], q_in, other_core)]
@@ -326,7 +343,10 @@
     c_in[z] = high
     c_copies = [send(c_in.at[z], c_in.at[z], d) for d in z_devices]
     for m in range(4):
-        dx[m, :, 0:128] = join(put(z3[m // 2], m % 2), put(z4, 1 - m // 2))
+        dx[m] = join(put(z3[m // 2], m % 2), put(z4, 1 - m // 2))
+    own_eight = pl.ds(pl.multiple_of(32 * j + 8 * x, 8), 8)
+    zt1[own_eight, :] = dx[x]
+    zt1_copies = [send(dx.at[m], zt1.at[own_eight, :], d) for m, d in plane_members]
     arrive(mzy_copies)
     mzc_copies = [
         send(mz.at[:, core_rows, :], mz.at[:, core_rows, :], other_core),
@@ -339,6 +359,13 @@
     arrive(mzc_copies)
     m5 = [jnp.concatenate([mz[2 * p], mz[2 * p + 1]], 0) for p in range(4)]
     m6 = [jnp.concatenate([mz[8 + 2 * n], mz[9 + 2 * n]], 0) for n in range(2)]
+    arrive(z0_copies)
+    arrive(zac_copies)
+    near = z0[1 - core]
+    far = z0[2]
+    own0 = jnp.concatenate([jnp.where(core == 0, near, far), jnp.where(core == 0, far, near)], 0)
+    update(slice(0, 128), zt0[...])
+    update(slice(384, 512), join(jnp.zeros_like(own0), own0))
     arrive(c_copies)
     low = [c_in[m, :, 0:128] for m in range(8)]
     top = [c_in[m, :, 128:] for m in range(8)]
@@ -362,36 +389,19 @@
     own6 = z6s[lax.div(z, 4)]
     own6 = jnp.where(side6 == 0, swap(own6), own6)
     own7 = jnp.where(side7 == 0, z7, swap(z7))
-    middle = join(own5, own6)
-    for m in range(4):
-        dx[m, :, 128:256] = middle
-        dx[m, :, 256:384] = own7
-
-    x_rows = rows_at(x, 8)
-    d_in[x_rows, :] = dx[x]
-    d_copies = [send(dx.at[m], d_in.at[x_rows, :], d) for m, d in zip(x_members, x_devices)]
-    arrive(d_copies)
-    ztb[own_cols, :] = d_in[...]
-    ztb_copies = [send(d_in, ztb.at[own_cols, :], d) for d in y_devices]
+    last = jnp.concatenate([join(own5, own6), join(own7, jnp.zeros_like(own7))], 1)
+
+    d_out[...] = last
+    ztb[own_eight, :] = last
+    ztb_copies = [send(d_out, ztb.at[own_eight, :], d) for _, d in plane_members]
+    arrive(zt1_copies)
+    zt1c_copies = [send(zt1.at[half_cols, :], zt1.at[half_cols, :], other_core)]
+    arrive(zt1c_copies)
+    update(slice(128, 256), zt1[...])
     arrive(ztb_copies)
     ztbc_copies = [send(ztb.at[half_cols, :], ztb.at[half_cols, :], other_core)]
-    arrive(z0_copies)
-    arrive(zac_copies)
     arrive(ztbc_copies)
-    near = z0[1 - core]
-    far = z0[2]
-    own0 = jnp.concatenate([jnp.where(core == 0, near, far), jnp.where(core == 0, far, near)], 0)
-    whole = jnp.concatenate([zt0[...], ztb[:, 0:256], join(ztb[:, 256:], own0)], 1).T
-    xh[:, 0:256], xl[:, 0:256] = split(whole)
-
-    def update(c, carry):
-        rows = rows_at(c, 512)
-        taken = dot3((uh[rows, :], ul[rows, :]), (xh[:, 0:256], xl[:, 0:256]))
-        field[0, rows, :] = field[0, rows, :] - taken[:, :128]
-        field[1, rows, :] = field[1, rows, :] - taken[:, 128:]
-        return carry
-
-    lax.fori_loop(0, 2, update, 0)
+    update(slice(256, 512), ztb[...])
     for copy in started:
         copy.wait_send()
     assert used[0] == COPIES
@@ -435,8 +445,8 @@
             h(512, 512), h(512, 512), h(512, 512), f(2, 1024, 128),
             h(1024, 256), h(1024, 256),
             f(256, 512), f(128, 512), f(128, 512), f(4, 32, 512), f(4, 32, 128), f(3, 128, 128),
-            f(32, 384), f(4, 8, 384), f(8, 8, 256), f(4, 8, 128), f(2, 8, 128), f(4, 8, 384),
-            f(32, 384), f(256, 128), f(256, 384),
+            f(32, 384), f(4, 8, 384), f(8, 8, 256), f(4, 8, 128), f(2, 8, 128), f(4, 8, 128),
+            f(8, 256), f(256, 128), f(256, 128), f(256, 256),
             f(2, 128, 128), f(2, 128, 128), f(4, 128, 128), f(2, 128, 128),
             f(512, 512), f(128, 512), f(2, 32, 384), f(4, 64, 384), f(4, 32, 384), f(2, 64, 384),
             f(64, 768), f(4, 8, 768), f(4, 8, 768), f(8, 8, 256), f(6, 64, 256), f(12, 64, 128),

time: 54.7 us -> 51.7 us (0.945)
  Pallas kernels: 54.6 us -> 51.6 us
    pallas_call x1, Pallas kernels: 53.1 us -> 50.1 us  [shards(): pl.pallas_call(solve_kernel, out_shape=pltpu.VMEM((2, 1024, 128), F32), i...]
where the time goes in v4:
time: 51.7 us; the launch traced here: 51.6 us
  Pallas kernels  51.6 us (100%)
    pallas_call x1, Pallas kernels, shards(): pl.pallas_call(solve_kernel, out_shape=pltpu.VMEM((2, 1024, 128), F32), i...  50.1 us
    pallas_call x1, Pallas kernels, shards(): pl.pallas_call(scatter_kernel, out_shape=jax.ShapeDtypeStruct((2048, 128)...  1.51 us

profile of v4, /device:TPU:1, one launch (start us, length us, event | category | flops | bytes accessed | tf_op | source)
XLA Modules:
  0.0 51.6 jit_solution(8392717679224646748)
XLA Ops:
  0.0 0.0 copy-start
  0.0 50.1 %shard_map.55.field = f32[2,1024,128]{2,1,0:T(8,128)S(1)} custom-call(f32[2048,128]{1,0:T(8,128)} %bitcast.14, s32[1,512]{1,0:T(1,128)} %bitcast.12, f32[1024,1024]{1,0:T(8,128)} %linv.1, f32[8,1024,128]{2,1,0:T(8,128)} %basis.1, f32[8,128,128]{2,1,0:T(8,128)} %bitcast.15), custom_call_target="tpu_custom_call" | custom-call | tf_op jit(solution)/shard_map/pallas_call | solution.py:436
  50.1 0.0 copy-done
  50.1 1.5 %shard_map.56 = f32[2048,128]{1,0:T(8,128)} custom-call(f32[2,1024,128]{2,1,0:T(8,128)S(1)} %shard_map.55.field, s32[1,512]{1,0:T(1,128)S(1)} %bitcast.13), custom_call_target="tpu_custom_call" | custom-call | tf_op jit(solution)/shard_map/pallas_call | solution.py:460
Async XLA Ops:
  0.0 50.1 %copy-start = (s32[512]{0:T(512)S(1)}, s32[512]{0:T(512)}, u32[]{:S(2)}) copy-start(s32[512]{0:T(512)} %param.6) | copy-start | bytes 6148

commit v5 on v4

--- a/solution.py
+++ b/solution.py
@@ -127,9 +127,6 @@
     cap_load = pltpu.make_async_copy(cap, cap_v, lsem.at[16])
     cap_load.start()
     rhs_load = pltpu.make_async_copy(rhs, rhs_v, lsem.at[17])
-    rhs_load.start()
-    for c in range(2):
-        linv_load(c).start()
 
     barrier = pltpu.get_barrier_semaphore()
     partners = [other_core] + [d for _, d in plane_members] + z_devices
@@ -139,6 +136,16 @@
     def pack(c, carry):
         rows = rows_at(c, 256)
         basis_load(c).wait()
+
+        @pl.when(c == 2)
+        def _():
+            rhs_load.start()
+
+        @pl.when(c == 3)
+        def _():
+            for part in range(2):
+                linv_load(part).start()
+
         for t in range(4):
             a = basis_v[PACKED[2 * t], rows, :]
             b = basis_v[PACKED[2 * t + 1], rows, :]
@@ -187,20 +194,7 @@
             cols = slice((2 * c + half) * 128, (2 * c + half) * 128 + 128)
             xh[:, cols], xl[:, cols] = split(rhs_v[pl.ds(2 * half + c, 512, stride=4), :])
 
-    arrive(g_copies[:1])
-    for level in range(2):
-        rows = pl.ds(pl.multiple_of(64 * level + 32 * core, 32), 32)
-        tiles = [gram[rows, low : low + 128] + g_in[rows, low : low + 128] for low in (0, 128, 256, 384)]
-        g12[level, :, 0:128] = join(tiles[3], tiles[0])
-        g12[level, :, 128:256] = tiles[1]
-        g12[level, :, 256:384] = tiles[2]
-    core_rows = rows_at(core, 32)
-    g1[y, core_rows, :] = g12[0]
-    g2r[y, :, :] = g12[1]
-    g1_copies = [send(g12.at[0], g1.at[y, core_rows, :], d) for d in y_devices]
-    g2_copies = [send(g12.at[1], g2r.at[y], d) for d in y_devices]
-
-    arrive(g_copies[1:])
+    arrive(g_copies)
     for at, base in ((0, 128), (256, 192)):
         rows = slice(base, base + 64)
         tiles = [gram[rows, low : low + 128] + g_in[rows, low : low + 128] for low in (128, 256, 384)]
@@ -215,6 +209,18 @@
         send(pk.at[rows_at(core * 4 + m, 8), :], pk_in.at[y], d) for m, d in zip(y_members, y_devices)
     ]
 
+    for level in range(2):
+        rows = pl.ds(pl.multiple_of(64 * level + 32 * core, 32), 32)
+        tiles = [gram[rows, low : low + 128] + g_in[rows, low : low + 128] for low in (0, 128, 256, 384)]
+        g12[level, :, 0:128] = join(tiles[3], tiles[0])
+        g12[level, :, 128:256] = tiles[1]
+        g12[level, :, 256:384] = tiles[2]
+    core_rows = rows_at(core, 32)
+    g1[y, core_rows, :] = g12[0]
+    g2r[y, :, :] = g12[1]
+    g1_copies = [send(g12.at[0], g1.at[y, core_rows, :], d) for d in y_devices]
+    g2_copies = [send(g12.at[1], g2r.at[y], d) for d in y_devices]
+
     for source, target in ((xh, oh), (xl, ol)):
         for b in range(4):
             moved = mm(pick[128 * b : 128 * b + 128, :], source[...])
@@ -253,11 +259,11 @@
     own_half = rows_at(core, 128)
     q_copies = [send(qraw.at[rows_at(1 - core, 128), :], q_in, other_core)]
     own_rows = rows_at(j, 8)
+    arrive(g0_copies)
+    arrive(q_copies)
     arrive(pk_copies)
     x4[x] = pk_in[0] + pk_in[1] + pk_in[2] + pk_in[3]
     x4_copies = [send(x4.at[x], x4.at[x], d) for d in x_devices]
-    arrive(g0_copies)
-    arrive(q_copies)
     mine, others = qraw[own_half, :], q_in[...]
     first = jnp.where(core == 0, mine[:, 384:], others[:, 384:])
     second = jnp.where(core == 0, others[:, 384:], mine[:, 384:])
@@ -286,13 +292,13 @@
         mx[m, own_rows, :] = x4[m, :, 0:256]
     for h in range(2):
         mx[4 + h, own_rows, :] = x4[2 * h, :, 256:512] + x4[2 * h + 1, :, 256:512]
+    mxy_copies = [send(mx.at[:, own_rows, :], mx.at[:, own_rows, :], d) for d in y_devices]
     z8[z] = x4[0, :, 512:] + x4[1, :, 512:] + x4[2, :, 512:] + x4[3, :, 512:]
     z8_copies = [send(z8.at[z], z8.at[z], d) for d in z_devices]
     arrive(g12c_copies)
     m1 = [jnp.concatenate([g1[2 * n], g1[2 * n + 1]], 0) for n in range(2)]
     m2 = jnp.concatenate([g2[0], g2[1]], 0)
     arrive(y_copies)
-    mxy_copies = [send(mx.at[:, own_rows, :], mx.at[:, own_rows, :], d) for d in y_devices]
     low = [y_in[m, :, 0:128] for m in range(4)]
     z1 = [product(join(low[2 * n + 1], swap(low[2 * n])), c1b[n], True) for n in range(2)]
     y1 = [product(z1[n], m1[n]) for n in range(2)]

time: 51.7 us -> 49 us (0.948)
  Pallas kernels: 51.6 us -> 48.9 us
    pallas_call x1, Pallas kernels: 50.1 us -> 47.4 us  [shards(): pl.pallas_call(solve_kernel, out_shape=pltpu.VMEM((2, 1024, 128), F32), i...]
where the time goes in v5:
time: 49 us; the launch traced here: 48.9 us
  Pallas kernels  48.9 us (100%)
    pallas_call x1, Pallas kernels, shards(): pl.pallas_call(solve_kernel, out_shape=pltpu.VMEM((2, 1024, 128), F32), i...  47.4 us
    pallas_call x1, Pallas kernels, shards(): pl.pallas_call(scatter_kernel, out_shape=jax.ShapeDtypeStruct((2048, 128)...  1.5 us

profile of v5, /device:TPU:1, one launch (start us, length us, event | category | flops | bytes accessed | tf_op | source)
XLA Modules:
  0.0 48.9 jit_solution(1706445274218389523)
XLA Ops:
  0.0 0.0 copy-start
  0.0 47.4 %shard_map.55.field = f32[2,1024,128]{2,1,0:T(8,128)S(1)} custom-call(f32[2048,128]{1,0:T(8,128)} %bitcast.14, s32[1,512]{1,0:T(1,128)} %bitcast.12, f32[1024,1024]{1,0:T(8,128)} %linv.1, f32[8,1024,128]{2,1,0:T(8,128)} %basis.1, f32[8,128,128]{2,1,0:T(8,128)} %bitcast.15), custom_call_target="tpu_custom_call" | custom-call | tf_op jit(solution)/shard_map/pallas_call | solution.py:442
  47.4 0.0 copy-done
  47.4 1.5 %shard_map.56 = f32[2048,128]{1,0:T(8,128)} custom-call(f32[2,1024,128]{2,1,0:T(8,128)S(1)} %shard_map.55.field, s32[1,512]{1,0:T(1,128)S(1)} %bitcast.13), custom_call_target="tpu_custom_call" | custom-call | tf_op jit(solution)/shard_map/pallas_call | solution.py:466
Async XLA Ops:
  0.0 47.4 %copy-start = (s32[512]{0:T(512)S(1)}, s32[512]{0:T(512)}, u32[]{:S(2)}) copy-start(s32[512]{0:T(512)} %param.6) | copy-start | bytes 6148

commit v6 on v5

--- a/solution.py
+++ b/solution.py
@@ -77,11 +77,11 @@
     row = plane + x * 8
     cell = y * 2 + core
 
-    y_members = [lax.rem(y + r, 4) for r in range(1, 4)]
+    y_members = [lax.rem(y + r, 4) for r in (2, 1, 3)]
     y_devices = [row + m * 2 + core for m in y_members]
-    x_members = [lax.rem(x + r, 4) for r in range(1, 4)]
+    x_members = [lax.rem(x + r, 4) for r in (2, 1, 3)]
     x_devices = [plane + m * 8 + cell for m in x_members]
-    z_members = [lax.rem(z + r, 8) for r in range(1, 8)]
+    z_members = [lax.rem(z + r, 8) for r in (4, 3, 5, 2, 6, 1, 7)]
     z_devices = [m * 32 + x * 8 + cell for m in z_members]
     other_core = row + y * 2 + (1 - core)
     plane_members = []
@@ -122,26 +122,41 @@
         rows = pl.ds(c * 512, 512)
         return pltpu.make_async_copy(linv.at[rows, :], linv_v.at[rows, :], lsem.at[8 + c])
 
+    rhs_load = pltpu.make_async_copy(rhs, rhs_v, lsem.at[17])
+    rhs_load.start()
     for c in range(4):
         basis_load(c).start()
     cap_load = pltpu.make_async_copy(cap, cap_v, lsem.at[16])
     cap_load.start()
-    rhs_load = pltpu.make_async_copy(rhs, rhs_v, lsem.at[17])
 
     barrier = pltpu.get_barrier_semaphore()
     partners = [other_core] + [d for _, d in plane_members] + z_devices
     for device in partners:
         pl.semaphore_signal(barrier, inc=1, device_id=(device,), device_id_type=MESH)
 
+    rhs_load.wait()
+    local = order[...] - me * 512
+    for b in range(4):
+        pick[:, 128 * b : 128 * b + 128] = one_hot(local, 128 * b, 128).T.astype(BF16)
+    for c in range(2):
+        for half in range(2):
+            cols = slice((2 * c + half) * 128, (2 * c + half) * 128 + 128)
+            xh[:, cols], xl[:, cols] = split(rhs_v[pl.ds(2 * half + c, 512, stride=4), :])
+    for source, target in ((xh, oh), (xl, ol)):
+        for b in range(4):
+            moved = mm(pick[128 * b : 128 * b + 128, :], source[...])
+            for c in range(2):
+                for half in range(2):
+                    at = (2 * c + half) * 128
+                    gathered[half, pl.ds(256 * b + c, 128, stride=2), :] = moved[:, at : at + 128]
+        for half in range(2):
+            target[:, 128 * half : 128 * half + 128] = gathered[half].astype(BF16)
+
     def pack(c, carry):
         rows = rows_at(c, 256)
         basis_load(c).wait()
 
         @pl.when(c == 2)
-        def _():
-            rhs_load.start()
-
-        @pl.when(c == 3)
         def _():
             for part in range(2):
                 linv_load(part).start()
@@ -178,21 +193,12 @@
     c3b[lax.div(x, 2)] = cap_v[3]
     c5b[lax.div(z, 2), eighths, :] = cap_v[5, eighths, :]
     c6b[lax.div(z, 4), eighths, :] = cap_v[6, eighths, :]
-    c1_copies = [send(cap_v.at[1, halves, :], c1b.at[lax.div(y, 2), halves, :], y_devices[1])]
-    c3_copies = [send(cap_v.at[3, halves, :], c3b.at[lax.div(x, 2), halves, :], x_devices[1])]
+    c1_copies = [send(cap_v.at[1, halves, :], c1b.at[lax.div(y, 2), halves, :], y_devices[0])]
+    c3_copies = [send(cap_v.at[3, halves, :], c3b.at[lax.div(x, 2), halves, :], x_devices[0])]
     c5_copies = [
-        send(cap_v.at[5, eighths, :], c5b.at[lax.div(z, 2), eighths, :], z_devices[r - 1]) for r in (2, 4, 6)
+        send(cap_v.at[5, eighths, :], c5b.at[lax.div(z, 2), eighths, :], z_devices[r]) for r in (0, 3, 4)
     ]
-    c6_copies = [send(cap_v.at[6, eighths, :], c6b.at[lax.div(z, 4), eighths, :], z_devices[3])]
-
-    rhs_load.wait()
-    local = order[...] - me * 512
-    for b in range(4):
-        pick[:, 128 * b : 128 * b + 128] = one_hot(local, 128 * b, 128).T.astype(BF16)
-    for c in range(2):
-        for half in range(2):
-            cols = slice((2 * c + half) * 128, (2 * c + half) * 128 + 128)
-            xh[:, cols], xl[:, cols] = split(rhs_v[pl.ds(2 * half + c, 512, stride=4), :])
+    c6_copies = [send(cap_v.at[6, eighths, :], c6b.at[lax.div(z, 4), eighths, :], z_devices[0])]
 
     arrive(g_copies)
     for at, base in ((0, 128), (256, 192)):
@@ -220,16 +226,6 @@
     g2r[y, :, :] = g12[1]
     g1_copies = [send(g12.at[0], g1.at[y, core_rows, :], d) for d in y_devices]
     g2_copies = [send(g12.at[1], g2r.at[y], d) for d in y_devices]
-
-    for source, target in ((xh, oh), (xl, ol)):
-        for b in range(4):
-            moved = mm(pick[128 * b : 128 * b + 128, :], source[...])
-            for c in range(2):
-                for half in range(2):
-                    at = (2 * c + half) * 128
-                    gathered[half, pl.ds(256 * b + c, 128, stride=2), :] = moved[:, at : at + 128]
-        for half in range(2):
-            target[:, 128 * half : 128 * half + 128] = gathered[half].astype(BF16)
 
     def leaf(c, carry):
         rows = rows_at(c, 512)

time: 49 us -> 49.1 us (level)
  no operation moved by 1% of the time
where the time goes in v6:
time: 49.1 us; the launch traced here: 49 us
  Pallas kernels  49 us (100%)
    pallas_call x1, Pallas kernels, shards(): pl.pallas_call(solve_kernel, out_shape=pltpu.VMEM((2, 1024, 128), F32), i...  47.5 us
    pallas_call x1, Pallas kernels, shards(): pl.pallas_call(scatter_kernel, out_shape=jax.ShapeDtypeStruct((2048, 128)...  1.5 us

profile of v6, /device:TPU:1, one launch (start us, length us, event | category | flops | bytes accessed | tf_op | source)
XLA Modules:
  0.0 49.0 jit_solution(6036941194967260769)
XLA Ops:
  0.0 0.0 copy-start
  0.0 47.5 %shard_map.55.field = f32[2,1024,128]{2,1,0:T(8,128)S(1)} custom-call(f32[2048,128]{1,0:T(8,128)} %bitcast.14, s32[1,512]{1,0:T(1,128)} %bitcast.12, f32[1024,1024]{1,0:T(8,128)} %linv.1, f32[8,1024,128]{2,1,0:T(8,128)} %basis.1, f32[8,128,128]{2,1,0:T(8,128)} %bitcast.15), custom_call_target="tpu_custom_call" | custom-call | tf_op jit(solution)/shard_map/pallas_call | solution.py:438
  47.5 0.0 copy-done
  47.5 1.5 %shard_map.56 = f32[2048,128]{1,0:T(8,128)} custom-call(f32[2,1024,128]{2,1,0:T(8,128)S(1)} %shard_map.55.field, s32[1,512]{1,0:T(1,128)S(1)} %bitcast.13), custom_call_target="tpu_custom_call" | custom-call | tf_op jit(solution)/shard_map/pallas_call | solution.py:462
Async XLA Ops:
  0.0 47.5 %copy-start = (s32[512]{0:T(512)S(1)}, s32[512]{0:T(512)}, u32[]{:S(2)}) copy-start(s32[512]{0:T(512)} %param.6) | copy-start | bytes 6148

commit v7 on v5

--- a/solution.py
+++ b/solution.py
@@ -77,11 +77,11 @@
     row = plane + x * 8
     cell = y * 2 + core
 
-    y_members = [lax.rem(y + r, 4) for r in range(1, 4)]
+    y_members = [lax.rem(y + r, 4) for r in (2, 1, 3)]
     y_devices = [row + m * 2 + core for m in y_members]
-    x_members = [lax.rem(x + r, 4) for r in range(1, 4)]
+    x_members = [lax.rem(x + r, 4) for r in (2, 1, 3)]
     x_devices = [plane + m * 8 + cell for m in x_members]
-    z_members = [lax.rem(z + r, 8) for r in range(1, 8)]
+    z_members = [lax.rem(z + r, 8) for r in (4, 3, 5, 2, 6, 1, 7)]
     z_devices = [m * 32 + x * 8 + cell for m in z_members]
     other_core = row + y * 2 + (1 - core)
     plane_members = []
@@ -159,12 +159,24 @@
 
     lax.fori_loop(0, 4, pack, 0)
 
+    pl.semaphore_wait(barrier, len(partners))
+    cap_load.wait()
+    halves, eighths = rows_at(core, 64), rows_at(j, 16)
+    c1b[lax.div(y, 2)] = cap_v[1]
+    c3b[lax.div(x, 2)] = cap_v[3]
+    c5b[lax.div(z, 2), eighths, :] = cap_v[5, eighths, :]
+    c6b[lax.div(z, 4), eighths, :] = cap_v[6, eighths, :]
+    c1_copies = [send(cap_v.at[1, halves, :], c1b.at[lax.div(y, 2), halves, :], y_devices[0])]
+    c3_copies = [send(cap_v.at[3, halves, :], c3b.at[lax.div(x, 2), halves, :], x_devices[0])]
+    c5_copies = [
+        send(cap_v.at[5, eighths, :], c5b.at[lax.div(z, 2), eighths, :], z_devices[r]) for r in (0, 3, 4)
+    ]
+    c6_copies = [send(cap_v.at[6, eighths, :], c6b.at[lax.div(z, 4), eighths, :], z_devices[0])]
+
     g_copies = []
     for t, low in ((0, 0), (3, 0), (1, 128), (2, 256)):
         rows = slice(128 * t, 128 * t + 128)
         gram[rows, low:] = dot3((uth[rows, :], utl[rows, :]), (wh[:, low:], wl[:, low:]))
-        if t == 0:
-            pl.semaphore_wait(barrier, len(partners))
         if t == 3:
             g0[rows_at(core, 64), :] = gram[448:512, :]
             g0_copies = [send(gram.at[pl.ds(448, 64), :], g0.at[rows_at(core, 64), :], other_core)]
@@ -172,19 +184,6 @@
             at = gram.at[pl.ds(128 * t, 128), pl.ds(low, 512 - low)]
             to = g_in.at[pl.ds(128 * t, 128), pl.ds(low, 512 - low)]
             g_copies.append(send(at, to, other_core))
-    cap_load.wait()
-    halves, eighths = rows_at(core, 64), rows_at(j, 16)
-    c1b[lax.div(y, 2)] = cap_v[1]
-    c3b[lax.div(x, 2)] = cap_v[3]
-    c5b[lax.div(z, 2), eighths, :] = cap_v[5, eighths, :]
-    c6b[lax.div(z, 4), eighths, :] = cap_v[6, eighths, :]
-    c1_copies = [send(cap_v.at[1, halves, :], c1b.at[lax.div(y, 2), halves, :], y_devices[1])]
-    c3_copies = [send(cap_v.at[3, halves, :], c3b.at[lax.div(x, 2), halves, :], x_devices[1])]
-    c5_copies = [
-        send(cap_v.at[5, eighths, :], c5b.at[lax.div(z, 2), eighths, :], z_devices[r - 1]) for r in (2, 4, 6)
-    ]
-    c6_copies = [send(cap_v.at[6, eighths, :], c6b.at[lax.div(z, 4), eighths, :], z_devices[3])]
-
     rhs_load.wait()
     local = order[...] - me * 512
     for b in range(4):

time: 49 us -> 48.9 us (level)
  no operation moved by 1% of the time
where the time goes in v7:
time: 48.9 us; the launch traced here: 48.8 us
  Pallas kernels  48.8 us (100%)
    pallas_call x1, Pallas kernels, shards(): pl.pallas_call(solve_kernel, out_shape=pltpu.VMEM((2, 1024, 128), F32), i...  47.2 us
    pallas_call x1, Pallas kernels, shards(): pl.pallas_call(scatter_kernel, out_shape=jax.ShapeDtypeStruct((2048, 128)...  1.5 us

profile of v7, /device:TPU:1, one launch (start us, length us, event | category | flops | bytes accessed | tf_op | source)
XLA Modules:
  0.0 48.8 jit_solution(2361577012138822661)
XLA Ops:
  0.0 0.0 copy-start
  0.0 47.2 %shard_map.55.field = f32[2,1024,128]{2,1,0:T(8,128)S(1)} custom-call(f32[2048,128]{1,0:T(8,128)} %bitcast.14, s32[1,512]{1,0:T(1,128)} %bitcast.12, f32[1024,1024]{1,0:T(8,128)} %linv.1, f32[8,1024,128]{2,1,0:T(8,128)} %basis.1, f32[8,128,128]{2,1,0:T(8,128)} %bitcast.15), custom_call_target="tpu_custom_call" | custom-call | tf_op jit(solution)/shard_map/pallas_call | solution.py:441
  47.3 0.0 copy-done
  47.3 1.5 %shard_map.56 = f32[2048,128]{1,0:T(8,128)} custom-call(f32[2,1024,128]{2,1,0:T(8,128)S(1)} %shard_map.55.field, s32[1,512]{1,0:T(1,128)S(1)} %bitcast.13), custom_call_target="tpu_custom_call" | custom-call | tf_op jit(solution)/shard_map/pallas_call | solution.py:465
Async XLA Ops:
  0.0 47.3 %copy-start = (s32[512]{0:T(512)S(1)}, s32[512]{0:T(512)}, u32[]{:S(2)}) copy-start(s32[512]{0:T(512)} %param.6) | copy-start | bytes 6148
